TPU v7x, 32 devices: a whole 2x2x4 slice. The times are simulated.
32 devices in a mesh: gx: 4 (over z), gy: 4 (over y, x), gz: 2 (over core).
Axes of the slice: x: 2, y: 2, z: 4, core: 2. Of those that a mesh axis runs over, the one named last changes fastest.
Arguments:
- u_old: float32 [3, 32, 32, 256], P(None, 'gx', 'gy', 'gz'), may hold values from -1.2 to 1.2
- u_trial: float32 [3, 32, 32, 256], P(None, 'gx', 'gy', 'gz'), may hold values from -3.6 to 3.6
- jacobian_inverse: float32 [3, 3, 32, 32, 256], P(None, None, 'gx', 'gy', 'gz'), may hold values from -0.6 to 1.5
- tile_base: int32 [2048], P(('gx', 'gy', 'gz')), may hold values from 0 to 63
- pair_codes: int32 [4, 2048, 128], P(None, ('gx', 'gy', 'gz')), may hold values from 0 to 127, as said below
- pair_groups: int32 [2048, 128], P(('gx', 'gy', 'gz')), may hold values from 0 to 2, as said below
Outputs:
- u_final: float32 [3, 32, 32, 256], P(None, 'gx', 'gy', 'gz')
- residual_norms: float32 [3], replicated
Inputs may be any that keep to these rules, and one draw needn't show every extreme that they name: `pair_groups`: on each device the tiles that hold a nonempty slot come first, and their first slot is never empty; every slot of the later tiles is 2. A device holds between 16 and 64 such tiles, and some device holds 64. `pair_codes`: Rows: first node 0 to 127, second direction 0 to 5, third offset 0 to 26, fourth direction 0 to 5; every node of a pair lies in the device's cells extended by one cell on every side.
All inputs are finite; a program needn't handle non-finite values.
Results may differ from a plain program's by a relative error of at most 0.0003.
Values sent between devices are 32-bit elements; how exact they have to be, the bound alone decides.
No kernel may reach another device: no remote copies, remote signals or barrier semaphores. Data moves between devices by JAX's collectives and lax.ppermute only.
A program may use at most 64 MiB of HBM per device.

v0:
```python
import jax
import jax.numpy as jnp
from jax import lax
from jax.sharding import PartitionSpec as P

ITERS = 3


step_size = 0.5
stiffness = 0.5
core_square = 0.5


def shifted(shard, axis, by):
    count = lax.axis_size(axis)
    pairs = [(i, i + by) for i in range(count) if 0 <= i + by < count]
    return lax.ppermute(shard, axis, pairs)


def padded_2(block, sides, width):
    for axis, dim in sides:
        count = lax.axis_size(axis)
        forward = [(i, i + 1) for i in range(count - 1)]
        backward = [(target, source) for source, target in forward]
        low = lax.ppermute(
            lax.slice_in_dim(block, block.shape[dim] - width, None, axis=dim), axis, forward
        )
        high = lax.ppermute(lax.slice_in_dim(block, 0, width, axis=dim), axis, backward)
        block = jnp.concatenate([low, block, high], axis=dim)
    return block


def unit_step(step_code):
    which_axis = step_code // 2
    direction = 1 - 2 * (step_code % 2)
    return [jnp.where(which_axis == k, direction, 0) for k in range(3)]


def pair_cells(tile_anchor, pair_code, blocks_y, blocks_z):
    anchor = tile_anchor[:, None]
    block_x = anchor // (blocks_y * blocks_z)
    block_y = anchor // blocks_z % blocks_y
    block_z = anchor % blocks_z
    inside = pair_code[0]
    first_node = [
        block_x * 4 + inside // 32 + 1,
        block_y * 4 + inside // 8 % 4 + 1,
        block_z * 8 + inside % 8 + 1,
    ]
    along_step = unit_step(pair_code[1])
    second_node = [first_node[k] + along_step[k] for k in range(3)]
    offset = pair_code[2]
    third_node = [
        first_node[0] + offset // 9 - 1,
        first_node[1] + offset // 3 % 3 - 1,
        first_node[2] + offset % 3 - 1,
    ]
    across_step = unit_step(pair_code[3])
    fourth_node = [third_node[k] + across_step[k] for k in range(3)]
    return [first_node, second_node, third_node, fourth_node]


def pair_terms(flat_u, node_cells, groups, frozen_too, flat_fn):
    points = []
    for node_cell in node_cells:
        lattice = jnp.stack(node_cell).astype(jnp.float32)
        points.append(lattice + flat_u[:, flat_fn(node_cell)])
    line_one = points[1] - points[0]
    line_two = points[3] - points[2]
    separation = 0.5 * (points[2] + points[3]) - 0.5 * (points[0] + points[1])
    square = jnp.sum(separation * separation, 0) + core_square
    coupling = stiffness * jnp.sum(line_one * line_two, 0) / (square * jnp.sqrt(square))
    push_force = coupling * separation
    pieces = [push_force * (groups == 0).astype(jnp.float32)]
    if frozen_too:
        pieces.append(push_force * (groups == 1).astype(jnp.float32))
    halves = 0.5 * jnp.concatenate(pieces, 0)
    return jnp.concatenate([-halves, -halves, halves, halves], 1)


def fold_back(summed):
    lower_face = shifted(summed[:, 0], "gx", -1)
    upper_face = shifted(summed[:, -1], "gx", 1)
    summed = summed[:, 1:-1].at[:, -1].add(lower_face).at[:, 0].add(upper_face)
    lower_face = shifted(summed[:, :, 0], "gy", -1)
    upper_face = shifted(summed[:, :, -1], "gy", 1)
    summed = summed[:, :, 1:-1].at[:, :, -1].add(lower_face).at[:, :, 0].add(upper_face)
    lower_face = shifted(summed[:, :, :, 0], "gz", -1)
    upper_face = shifted(summed[:, :, :, -1], "gz", 1)
    return summed[:, :, :, 1:-1].at[:, :, :, -1].add(lower_face).at[:, :, :, 0].add(upper_face)


def per_device(u_old, u_trial, jacobian_inverse, tile_base, pair_codes, pair_groups):
    size_x = u_old.shape[1]
    size_y = u_old.shape[2]
    size_z = u_old.shape[3]
    tile_count = tile_base.shape[0]
    per_block = max(1, tile_count // 16)
    blocks_y = size_y // 4
    blocks_z = size_z // 8
    width_y = size_y + 2
    width_z = size_z + 2
    cell_total = (
        3.0
        * size_x
        * size_y
        * size_z
        * lax.axis_size("gx")
        * lax.axis_size("gy")
        * lax.axis_size("gz")
    )
    live_tiles = jnp.sum(jnp.any(pair_groups < 2, axis=1).astype(jnp.int32))

    def flat_fn(node_cell):
        return (node_cell[0] * width_y + node_cell[1]) * width_z + node_cell[2]

    def accumulate(padded, tile_anchor, pair_code, groups, tile_live, frozen_too):
        flat_u = padded.reshape(3, -1)
        channels = 6 if frozen_too else 3
        tile_index = lax.broadcasted_iota(jnp.int32, groups.shape, 0)
        groups = jnp.where(tile_index < tile_live, groups, 2)

        def one_block(block_turn, summed):
            begin_at = block_turn * per_block
            anchor_part = lax.dynamic_slice_in_dim(tile_anchor, begin_at, per_block, 0)
            code_part = lax.dynamic_slice_in_dim(pair_code, begin_at, per_block, 1)
            group_part = lax.dynamic_slice_in_dim(groups, begin_at, per_block, 0)
            node_cells = pair_cells(anchor_part, code_part, blocks_y, blocks_z)
            values = pair_terms(flat_u, node_cells, group_part, frozen_too, flat_fn)
            flat_index = jnp.concatenate([flat_fn(node_cell) for node_cell in node_cells], 0)
            return summed.at[:, flat_index.reshape(-1)].add(values.reshape(channels, -1))

        block_turns = (tile_live + per_block - 1) // per_block
        initial = jnp.zeros((channels, flat_u.shape[1]), jnp.float32)
        summed = lax.fori_loop(0, block_turns, one_block, initial)
        return summed.reshape(channels, size_x + 2, width_y, width_z)

    def forces(current, frozen_too):
        padded = padded_2(current, (("gx", 1), ("gy", 2), ("gz", 3)), 1)
        summed = accumulate(padded, tile_base, pair_codes, pair_groups, live_tiles, frozen_too)
        return fold_back(summed)

    current = u_trial
    all_forces = forces(current, True)
    frozen = all_forces[3:]
    force_sum = all_forces[:3] + frozen
    square_list = []
    for iteration in range(ITERS):
        if iteration > 0:
            force_sum = forces(current, False) + frozen
        residual = current - u_old - step_size * force_sum
        local_square = jnp.sum(residual * residual)
        square_list.append(local_square)
        applied = [sum((jacobian_inverse[r, m] * residual[m] for m in range(3))) for r in range(3)]
        current = current - jnp.stack(applied)
    squares_all = lax.psum(jnp.stack(square_list), ("gx", "gy", "gz"))
    residual_norms = jnp.sqrt(squares_all / cell_total)
    return (current, residual_norms)


def solution(mesh):
    return jax.shard_map(
        per_device,
        mesh=mesh,
        in_specs=(
            P(None, "gx", "gy", "gz"),
            P(None, "gx", "gy", "gz"),
            P(None, None, "gx", "gy", "gz"),
            P(("gx", "gy", "gz")),
            P(None, ("gx", "gy", "gz"), None),
            P(("gx", "gy", "gz"), None),
        ),
        out_specs=(P(None, "gx", "gy", "gz"), P()),
        check_vma=False,
    )
```

profile of v0, /device:TPU:0, one launch (start us, length us, event | category | flops | bytes accessed | tf_op | source)
XLA Modules:
  0.0 1819.9 jit_solution(2830983238625153464)
XLA Ops:
  1.4 4.9 collective-permute-start
  26.6 4.2 copy.159
  33.8 334.3 %while.57 = (s32[]{:T(128)}, f32[6,13000]{0,1:T(8,128)}, s32[]{:T(128)}, s32[64]{0:T(128)S(1)}, s32[4,64,128]{2,1,0:T(8,128)S(1)}, /*index=5*/f32[3,13000]{0,1:T...) while((s32[]{:T(128)}, f32[6,13000]{0,1:T(8,128)}, ...), condition=%wide.region_6.7_spmd, body=%wide.region_2.6_spmd.sunk | while | flops 417477 | bytes 766047 | solution.py:135
  51.2 16.0 scatter_fusion
  84.6 16.0 scatter_fusion
  105.2 3.9 gather_fusion.3
  118.1 16.0 scatter_fusion
  151.5 16.0 scatter_fusion
  184.9 16.0 scatter_fusion
  218.4 16.0 scatter_fusion
  251.8 16.0 scatter_fusion
  285.2 16.0 scatter_fusion
  305.8 3.9 gather_fusion.3
  318.7 16.0 scatter_fusion
  352.1 16.0 scatter_fusion
  368.1 4.6 copy.160
  374.7 4.6 collective-permute-start.7
  383.0 4.5 collective-permute-start.9
  393.6 68.1 %collective-permute-start.11 = (f32[6,8,8]{2,1,0:T(8,128)S(1)}, f32[6,8,8]{2,1,0:T(8,128)S(1)}, u32[]{:S(2)}, u32[]{:S(2)}) collective-permute-start(f32[6,8,8]{2,1,0:T(8,128)S(1)} %get-tuple-element.766), channel_id=1, source_target_pairs={{0,1},{2,3},{4,5},{6,7},{8,9},{10,11},{12,13},{14,15},{16,17},{18,... | collective-permute-start | bytes 4616 | tf_op jit(solution)/shard_map/ppermute | solution.py:17
  467.4 38.3 %collective-permute-start.12 = (f32[3,1,8,128]{3,2,1,0:T(8,128)S(1)}, f32[3,1,8,128]{3,2,1,0:T(8,128)S(1)}, u32[]{:S(2)}, u32[]{:S(2)}) collective-permute-start(f32[3,1,8,128]{3,2,1,0:T(8,128)S(1)} %get-tuple-element.980), channel_id=1, source_target_pairs={{0,8},{8,16},{16,24},{1,9},{9,17},{17,25},{2,10},{10,18},{18,26},{... | collective-permute-start | bytes 36872 | tf_op jit(solution)/shard_map/ppermute | solution.py:25
  507.0 4.6 collective-permute-done.13
  511.7 36.7 %collective-permute-start.14 = (f32[3,10,1,128]{3,2,1,0:T(1,128)S(1)}, f32[3,10,1,128]{3,2,1,0:T(1,128)S(1)}, u32[]{:S(2)}, u32[]{:S(2)}) collective-permute-start(f32[3,10,1,128]{3,2,1,0:T(1,128)S(1)} %get-tuple-element.974), channel_id=1, source_target_pairs={{0,2},{2,4},{4,6},{1,3},{3,5},{5,7},{8,10},{10,12},{12,14},{9,11},... | collective-permute-start | bytes 46088 | tf_op jit(solution)/shard_map/ppermute | solution.py:25
  549.8 66.3 %collective-permute-done.15 = f32[3,10,1,128]{3,2,1,0:T(1,128)S(1)} collective-permute-done((f32[3,10,1,128]{3,2,1,0:T(1,128)S(1)}, f32[3,10,1,128]{3,2,1,0:T(1,128)S(1)}, u32[]{:S(2)}, u32[]{:S(2)}) %collective-permute-start.15) | collective-permute-done | bytes 15392 | tf_op jit(solution)/shard_map/ppermute | solution.py:28
  621.7 4.2 copy.170
  629.0 334.1 %while.58 = (s32[]{:T(128)}, f32[3,13000]{0,1:T(8,128)}, s32[]{:T(128)}, s32[64]{0:T(128)S(1)}, s32[4,64,128]{2,1,0:T(8,128)S(1)}, /*index=5*/f32[3,13000]{0,1:T...) while((s32[]{:T(128)}, f32[3,13000]{0,1:T(8,128)}, ...), condition=%wide.region_11.12_spmd, body=%wide.region_7.11_spmd.sunk | while | flops 384197 | bytes 565343 | solution.py:135
  646.3 16.0 scatter_fusion.1
  679.7 16.0 scatter_fusion.1
  700.3 3.9 gather_fusion.7
  713.1 16.0 scatter_fusion.1
  746.6 16.0 scatter_fusion.1
  780.0 16.0 scatter_fusion.1
  813.4 16.0 scatter_fusion.1
  846.8 16.0 scatter_fusion.1
  880.2 16.0 scatter_fusion.1
  900.7 3.9 gather_fusion.7
  913.6 16.0 scatter_fusion.1
  947.0 16.0 scatter_fusion.1
  963.1 4.6 copy.171
  969.3 4.5 collective-permute-start.19
  977.0 4.5 collective-permute-start.21
  984.9 67.6 %collective-permute-start.23 = (f32[3,8,8]{2,1,0:T(8,128)S(1)}, f32[3,8,8]{2,1,0:T(8,128)S(1)}, u32[]{:S(2)}, u32[]{:S(2)}) collective-permute-start(f32[3,8,8]{2,1,0:T(8,128)S(1)} %get-tuple-element.770), channel_id=1, source_target_pairs={{0,1},{2,3},{4,5},{6,7},{8,9},{10,11},{12,13},{14,15},{16,17},{18,... | collective-permute-start | bytes 2312 | tf_op jit(solution)/shard_map/ppermute | solution.py:17
  1056.2 37.4 %collective-permute-start.24 = (f32[3,1,8,128]{3,2,1,0:T(8,128)S(1)}, f32[3,1,8,128]{3,2,1,0:T(8,128)S(1)}, u32[]{:S(2)}, u32[]{:S(2)}) collective-permute-start(f32[3,1,8,128]{3,2,1,0:T(8,128)S(1)} %get-tuple-element.978), channel_id=1, source_target_pairs={{0,8},{8,16},{16,24},{1,9},{9,17},{17,25},{2,10},{10,18},{18,26},{... | collective-permute-start | bytes 36872 | tf_op jit(solution)/shard_map/ppermute | solution.py:25
  1095.0 4.5 collective-permute-done.25
  1099.6 38.1 %collective-permute-start.26 = (f32[3,10,1,128]{3,2,1,0:T(1,128)S(1)}, f32[3,10,1,128]{3,2,1,0:T(1,128)S(1)}, u32[]{:S(2)}, u32[]{:S(2)}) collective-permute-start(f32[3,10,1,128]{3,2,1,0:T(1,128)S(1)} %get-tuple-element.972), channel_id=1, source_target_pairs={{0,2},{2,4},{4,6},{1,3},{3,5},{5,7},{8,10},{10,12},{12,14},{9,11},... | collective-permute-start | bytes 46088 | tf_op jit(solution)/shard_map/ppermute | solution.py:25
  1139.1 65.3 %collective-permute-done.27 = f32[3,10,1,128]{3,2,1,0:T(1,128)S(1)} collective-permute-done((f32[3,10,1,128]{3,2,1,0:T(1,128)S(1)}, f32[3,10,1,128]{3,2,1,0:T(1,128)S(1)}, u32[]{:S(2)}, u32[]{:S(2)}) %collective-permute-start.27) | collective-permute-done | bytes 15392 | tf_op jit(solution)/shard_map/ppermute | solution.py:28
  1209.9 4.2 copy.180
  1217.2 334.1 %while.59 = (s32[]{:T(128)}, f32[3,13000]{0,1:T(8,128)}, s32[]{:T(128)}, s32[64]{0:T(128)S(1)}, s32[4,64,128]{2,1,0:T(8,128)S(1)}, /*index=5*/f32[3,13000]{0,1:T...) while((s32[]{:T(128)}, f32[3,13000]{0,1:T(8,128)}, ...), condition=%wide.region_16.17_spmd, body=%wide.region_12.16_spmd.sunk | while | flops 384197 | bytes 565343 | solution.py:135
  1234.5 16.0 scatter_fusion.2
  1268.0 16.0 scatter_fusion.2
  1288.5 3.9 gather_fusion.11
  1301.4 16.0 scatter_fusion.2
  1334.8 16.0 scatter_fusion.2
  1368.2 16.0 scatter_fusion.2
  1401.6 16.0 scatter_fusion.2
  1435.0 16.0 scatter_fusion.2
  1468.4 16.0 scatter_fusion.2
  1489.0 3.9 gather_fusion.11
  1501.8 16.0 scatter_fusion.2
  1535.3 16.0 scatter_fusion.2
  1551.3 4.6 copy.181
  1557.5 4.5 collective-permute-start.31
  1565.2 4.5 collective-permute-start.33
  1573.1 67.6 %collective-permute-start.35 = (f32[3,8,8]{2,1,0:T(8,128)S(1)}, f32[3,8,8]{2,1,0:T(8,128)S(1)}, u32[]{:S(2)}, u32[]{:S(2)}) collective-permute-start(f32[3,8,8]{2,1,0:T(8,128)S(1)} %get-tuple-element.768), channel_id=1, source_target_pairs={{0,1},{2,3},{4,5},{6,7},{8,9},{10,11},{12,13},{14,15},{16,17},{18,... | collective-permute-start | bytes 2312 | tf_op jit(solution)/shard_map/ppermute | solution.py:17
  1646.3 172.4 %psum.7 = f32[3]{0:T(128)S(1)} all-reduce(f32[3]{0:T(128)S(1)} %pad_maximum_fusion.15), channel_id=1, replica_groups=mesh['gx'=4,'gy'=4,'gz'=2] {'gx','gy','gz'}, use_global_device_ids=true, to_apply=%region_20.21 | all-reduce | flops 3 | bytes 24 | tf_op jit(solution)/shard_map/psum | solution.py:156
  (1041 shorter events, 584.4 us)
Async XLA Ops:
  1.4 7.8 collective-permute-start
  6.3 5.6 collective-permute-start.1
  11.9 5.4 collective-permute-start.2
  15.3 5.6 collective-permute-start.3
  21.1 4.1 collective-permute-start.4
  22.4 3.4 collective-permute-start.5
  26.5 7.3 copy-start.2
  26.6 7.3 copy-start.4
  368.1 98.5 %copy-start = (f32[3,8,8,128]{3,2,1,0:T(8,128)S(1)}, f32[3,8,8,128]{3,2,1,0:T(8,128)}, u32[]{:S(2)}) copy-start(f32[3,8,8,128]{3,2,1,0:T(8,128)} %param.49) | copy-start | bytes 294916
  368.1 98.5 %copy-start.3 = (f32[3,8,8,128]{3,2,1,0:T(8,128)S(1)}, f32[3,8,8,128]{3,2,1,0:T(8,128)}, u32[]{:S(2)}) copy-start(f32[3,8,8,128]{3,2,1,0:T(8,128)} %param.48) | copy-start | bytes 294916
  368.1 99.2 %copy-start.1 = (f32[3,3,8,8,128]{4,3,2,1,0:T(8,128)S(1)}, f32[3,3,8,8,128]{4,3,2,1,0:T(8,128)}, u32[]{:S(2)}) copy-start(f32[3,3,8,8,128]{4,3,2,1,0:T(8,128)} %param.50) | copy-start | bytes 884740
  373.3 6.5 collective-permute-start.6
  374.7 6.8 collective-permute-start.7
  381.6 6.0 collective-permute-start.8
  383.0 6.8 collective-permute-start.9
  392.1 69.5 %collective-permute-start.10 = (f32[6,8,8]{2,1,0:T(8,128)S(1)}, f32[6,8,8]{2,1,0:T(8,128)S(1)}, u32[]{:S(2)}, u32[]{:S(2)}) collective-permute-start(f32[6,8,8]{2,1,0:T(8,128)S(1)} %get-tuple-element.767), channel_id=1, source_target_pairs={{1,0},{3,2},{5,4},{7,6},{9,8},{11,10},{13,12},{15,14},{17,16},{19,... | collective-permute-start | bytes 4616 | tf_op jit(solution)/shard_map/ppermute | solution.py:17
  393.6 68.9 %collective-permute-start.11 = (f32[6,8,8]{2,1,0:T(8,128)S(1)}, f32[6,8,8]{2,1,0:T(8,128)S(1)}, u32[]{:S(2)}, u32[]{:S(2)}) collective-permute-start(f32[6,8,8]{2,1,0:T(8,128)S(1)} %get-tuple-element.766), channel_id=1, source_target_pairs={{0,1},{2,3},{4,5},{6,7},{8,9},{10,11},{12,13},{14,15},{16,17},{18,... | collective-permute-start | bytes 4616 | tf_op jit(solution)/shard_map/ppermute | solution.py:17
  467.4 39.7 %collective-permute-start.12 = (f32[3,1,8,128]{3,2,1,0:T(8,128)S(1)}, f32[3,1,8,128]{3,2,1,0:T(8,128)S(1)}, u32[]{:S(2)}, u32[]{:S(2)}) collective-permute-start(f32[3,1,8,128]{3,2,1,0:T(8,128)S(1)} %get-tuple-element.980), channel_id=1, source_target_pairs={{0,8},{8,16},{16,24},{1,9},{9,17},{17,25},{2,10},{10,18},{18,26},{... | collective-permute-start | bytes 36872 | tf_op jit(solution)/shard_map/ppermute | solution.py:25
  505.7 6.0 collective-permute-start.13
  511.7 38.2 %collective-permute-start.14 = (f32[3,10,1,128]{3,2,1,0:T(1,128)S(1)}, f32[3,10,1,128]{3,2,1,0:T(1,128)S(1)}, u32[]{:S(2)}, u32[]{:S(2)}) collective-permute-start(f32[3,10,1,128]{3,2,1,0:T(1,128)S(1)} %get-tuple-element.974), channel_id=1, source_target_pairs={{0,2},{2,4},{4,6},{1,3},{3,5},{5,7},{8,10},{10,12},{12,14},{9,11},... | collective-permute-start | bytes 46088 | tf_op jit(solution)/shard_map/ppermute | solution.py:25
  548.4 67.7 %collective-permute-start.15 = (f32[3,10,1,128]{3,2,1,0:T(1,128)S(1)}, f32[3,10,1,128]{3,2,1,0:T(1,128)S(1)}, u32[]{:S(2)}, u32[]{:S(2)}) collective-permute-start(f32[3,10,1,128]{3,2,1,0:T(1,128)S(1)} %get-tuple-element.975), channel_id=1, source_target_pairs={{2,0},{4,2},{6,4},{3,1},{5,3},{7,5},{10,8},{12,10},{14,12},{11,9},... | collective-permute-start | bytes 46088 | tf_op jit(solution)/shard_map/ppermute | solution.py:28
  616.3 2.8 collective-permute-start.16
  617.6 3.4 collective-permute-start.17
  968.0 6.0 collective-permute-start.18
  969.3 6.3 collective-permute-start.19
  975.7 5.9 collective-permute-start.20
  977.0 6.1 collective-permute-start.21
  983.5 69.0 %collective-permute-start.22 = (f32[3,8,8]{2,1,0:T(8,128)S(1)}, f32[3,8,8]{2,1,0:T(8,128)S(1)}, u32[]{:S(2)}, u32[]{:S(2)}) collective-permute-start(f32[3,8,8]{2,1,0:T(8,128)S(1)} %get-tuple-element.771), channel_id=1, source_target_pairs={{1,0},{3,2},{5,4},{7,6},{9,8},{11,10},{13,12},{15,14},{17,16},{19,... | collective-permute-start | bytes 2312 | tf_op jit(solution)/shard_map/ppermute | solution.py:17
  984.9 68.4 %collective-permute-start.23 = (f32[3,8,8]{2,1,0:T(8,128)S(1)}, f32[3,8,8]{2,1,0:T(8,128)S(1)}, u32[]{:S(2)}, u32[]{:S(2)}) collective-permute-start(f32[3,8,8]{2,1,0:T(8,128)S(1)} %get-tuple-element.770), channel_id=1, source_target_pairs={{0,1},{2,3},{4,5},{6,7},{8,9},{10,11},{12,13},{14,15},{16,17},{18,... | collective-permute-start | bytes 2312 | tf_op jit(solution)/shard_map/ppermute | solution.py:17
  1056.2 38.8 %collective-permute-start.24 = (f32[3,1,8,128]{3,2,1,0:T(8,128)S(1)}, f32[3,1,8,128]{3,2,1,0:T(8,128)S(1)}, u32[]{:S(2)}, u32[]{:S(2)}) collective-permute-start(f32[3,1,8,128]{3,2,1,0:T(8,128)S(1)} %get-tuple-element.978), channel_id=1, source_target_pairs={{0,8},{8,16},{16,24},{1,9},{9,17},{17,25},{2,10},{10,18},{18,26},{... | collective-permute-start | bytes 36872 | tf_op jit(solution)/shard_map/ppermute | solution.py:25
  1093.6 5.9 collective-permute-start.25
  1099.6 39.5 %collective-permute-start.26 = (f32[3,10,1,128]{3,2,1,0:T(1,128)S(1)}, f32[3,10,1,128]{3,2,1,0:T(1,128)S(1)}, u32[]{:S(2)}, u32[]{:S(2)}) collective-permute-start(f32[3,10,1,128]{3,2,1,0:T(1,128)S(1)} %get-tuple-element.972), channel_id=1, source_target_pairs={{0,2},{2,4},{4,6},{1,3},{3,5},{5,7},{8,10},{10,12},{12,14},{9,11},... | collective-permute-start | bytes 46088 | tf_op jit(solution)/shard_map/ppermute | solution.py:25
  1137.6 66.7 %collective-permute-start.27 = (f32[3,10,1,128]{3,2,1,0:T(1,128)S(1)}, f32[3,10,1,128]{3,2,1,0:T(1,128)S(1)}, u32[]{:S(2)}, u32[]{:S(2)}) collective-permute-start(f32[3,10,1,128]{3,2,1,0:T(1,128)S(1)} %get-tuple-element.973), channel_id=1, source_target_pairs={{2,0},{4,2},{6,4},{3,1},{5,3},{7,5},{10,8},{12,10},{14,12},{11,9},... | collective-permute-start | bytes 46088 | tf_op jit(solution)/shard_map/ppermute | solution.py:28
  1204.5 2.6 collective-permute-start.28
  1205.8 3.4 collective-permute-start.29
  1556.2 6.0 collective-permute-start.30
  1557.5 6.3 collective-permute-start.31
  1563.9 5.9 collective-permute-start.32
  1565.2 6.1 collective-permute-start.33
  1571.7 69.0 %collective-permute-start.34 = (f32[3,8,8]{2,1,0:T(8,128)S(1)}, f32[3,8,8]{2,1,0:T(8,128)S(1)}, u32[]{:S(2)}, u32[]{:S(2)}) collective-permute-start(f32[3,8,8]{2,1,0:T(8,128)S(1)} %get-tuple-element.769), channel_id=1, source_target_pairs={{1,0},{3,2},{5,4},{7,6},{9,8},{11,10},{13,12},{15,14},{17,16},{19,... | collective-permute-start | bytes 2312 | tf_op jit(solution)/shard_map/ppermute | solution.py:17
  1573.1 68.5 %collective-permute-start.35 = (f32[3,8,8]{2,1,0:T(8,128)S(1)}, f32[3,8,8]{2,1,0:T(8,128)S(1)}, u32[]{:S(2)}, u32[]{:S(2)}) collective-permute-start(f32[3,8,8]{2,1,0:T(8,128)S(1)} %get-tuple-element.768), channel_id=1, source_target_pairs={{0,1},{2,3},{4,5},{6,7},{8,9},{10,11},{12,13},{14,15},{16,17},{18,... | collective-permute-start | bytes 2312 | tf_op jit(solution)/shard_map/ppermute | solution.py:17
where the time goes:
time: 1840 us; the launch traced here: 1820 us
  local copies, waits for them, and re-layouts  550 us (30%)
  other arithmetic  515 us (28%)
  starting transfers between devices  417 us (23%)
  blocking collectives  172 us (9%)
  waiting for transfers between devices  161 us (9%)
    gather x240, local copies, waits for them, and re-layouts, pair_terms(): points.append(lattice + flat_u[:, flat_fn(node_cell)])  484 us
    scatter-add x30, other arithmetic, one_block(): summed.at[:, flat_index.reshape(-1)].add(values.reshape(channels, -1))  481 us
    ppermute x18, starting transfers between devices, shifted(): return lax.ppermute(shard, axis, pairs)  242 us
    psum x1, blocking collectives, per_device(): squares_all = lax.psum(jnp.stack(square_list), ('gx', 'gy', 'gz'))  172 us
    ppermute x9, starting transfers between devices, padded_2(): lax.ppermute(lax.slice_in_dim(block, block.shape[dim] - width, None, axis...  163 us
    ppermute x9, waiting for transfers between devices, padded_2(): lax.ppermute(lax.slice_in_dim(block, 0, width, axis=dim), axis, backward)  151 us
  transfers between devices with their start and end apart: 36, of which 25 were waited for; matrix products, arithmetic and copies ran while one was open for 0% of the time, Pallas kernels for 0%

commit v1 on v0

v1 whole, which is shorter than its diff:
```python
import functools

import jax
import jax.numpy as jnp
from jax import lax
from jax.experimental import pallas as pl
from jax.experimental.pallas import tpu as pltpu
from jax.sharding import PartitionSpec as P

ITERS = 3
step_size = 0.5
stiffness = 0.5
core_square = 0.5

F32 = jnp.float32
BF16 = jnp.bfloat16
GROUP = 8


class Geo:
    def __init__(self, sx, sy, sz, tiles):
        self.sx, self.sy, self.sz, self.tiles = sx, sy, sz, tiles
        self.X, self.Y = sx + 2, sy + 2
        self.XY = self.X * self.Y
        self.LP = -(-self.XY // 128) * 128
        self.RP = -(-self.XY // 8) * 8
        self.ZR = sz + 8
        self.by = sy // 4
        self.bz = sz // 8
        self.slab = -(-(2 * max(self.X, self.Y) + 2) // 8) * 8


def roll(x, shift, size):
    return pltpu.roll(x, shift % size, 1)


def lane_xy(geo, shape):
    lane = lax.broadcasted_iota(jnp.int32, shape, len(shape) - 1)
    x = jnp.zeros_like(lane)
    for k in range(1, geo.X):
        x = x + (lane >= k * geo.Y).astype(jnp.int32)
    return lane, x, lane - x * geo.Y


def add_rows_x(geo, rows, low, high, has_low, has_high):
    lane, _, _ = lane_xy(geo, rows.shape)
    span = geo.sx * geo.Y
    from_low = roll(low, -span, geo.LP)
    from_high = roll(high, span, geo.LP)
    rows = rows + jnp.where((lane < 2 * geo.Y) & has_low, from_low, 0.0)
    return rows + jnp.where((lane >= span) & (lane < geo.XY) & has_high, from_high, 0.0)


def add_rows_y(geo, rows, low, high, has_low, has_high):
    lane, _, y = lane_xy(geo, rows.shape)
    from_low = roll(low, -geo.sy, geo.LP)
    from_high = roll(high, geo.sy, geo.LP)
    inside = lane < geo.XY
    rows = rows + jnp.where((y < 2) & inside & has_low, from_low, 0.0)
    return rows + jnp.where((y >= geo.sy) & inside & has_high, from_high, 0.0)


def fill_z_kernel(geo, ut, uo, ji, face, zbuf, wide):
    wide[...] = jnp.zeros_like(wide)
    zbuf[...] = jnp.zeros_like(zbuf)
    sources = [ut.at[c] for c in range(3)] + [uo.at[c] for c in range(3)] + [ji.at[c] for c in range(9)]
    for c, source in enumerate(sources):
        for x in range(geo.sx):
            start = (x + 1) * geo.Y + 1
            wide[start : start + geo.sy, :] = source[x * geo.sy : (x + 1) * geo.sy, :]
        value = wide[...]
        face[c] = value[: geo.RP]
        turned = value.T
        zbuf[c : c + 1, :] = turned[0:1]
        zbuf[16 + c : 17 + c, :] = turned[geo.sz - 1 : geo.sz]


def fill_rows(flags, z_low, z_high):
    low = jnp.where(flags[4] > 0, z_low[16:32, :], 0.0)
    high = jnp.where(flags[5] > 0, z_high[0:16, :], 0.0)
    return jnp.concatenate([low, high], 0)


def fill_x_kernel(geo, flags, ut, uo, ji, z_low, z_high, x_low, x_high):
    rows = fill_rows(flags, z_low, z_high)
    count = 15 * geo.sy
    sources = [ut.at[c] for c in range(3)] + [uo.at[c] for c in range(3)] + [ji.at[c] for c in range(9)]
    last = (geo.sx - 1) * geo.sy
    for c, source in enumerate(sources):
        x_low[c * geo.sy : (c + 1) * geo.sy, :] = source[0 : geo.sy, :]
        x_high[c * geo.sy : (c + 1) * geo.sy, :] = source[last : last + geo.sy, :]
    x_low[count : count + 32, :] = rows
    x_high[count : count + 32, :] = rows


def fill_y_kernel(geo, flags, face, z_low, z_high, from_low, from_high, out, rows_out, y_low, y_high):
    has_low, has_high = flags[0] > 0, flags[1] > 0
    count = 15 * geo.sy
    rows = add_rows_x(
        geo,
        fill_rows(flags, z_low, z_high),
        from_low[count : count + 32, :],
        from_high[count : count + 32, :],
        has_low,
        has_high,
    )
    rows_out[...] = rows
    out[...] = face[...]
    y_low[...] = jnp.zeros_like(y_low)
    y_high[...] = jnp.zeros_like(y_high)
    top = (geo.sx + 1) * geo.Y + 1
    for c in range(15):
        part = slice(c * geo.sy, (c + 1) * geo.sy)
        out[c, 1 : 1 + geo.sy, :] = jnp.where(has_low, from_low[part, :], 0.0)
        out[c, top : top + geo.sy, :] = jnp.where(has_high, from_high[part, :], 0.0)
        into = slice(c * geo.X, (c + 1) * geo.X)
        y_low[into, :] = out[c, pl.ds(1, geo.X, stride=geo.Y), :]
        y_high[into, :] = out[c, pl.ds(geo.sy, geo.X, stride=geo.Y), :]
    tail = fill_y_rows(geo) - 32
    y_low[tail : tail + 32, :] = rows
    y_high[tail : tail + 32, :] = rows


def fill_y_rows(geo):
    return -(-15 * geo.X // 8) * 8 + 32


def fill_done(geo, flags, face, rows_in, from_low, from_high, wide, targets):
    has_low, has_high = flags[2] > 0, flags[3] > 0
    tail = fill_y_rows(geo) - 32
    rows = add_rows_y(
        geo,
        rows_in[...],
        from_low[tail : tail + 32, :],
        from_high[tail : tail + 32, :],
        has_low,
        has_high,
    )
    wide[...] = jnp.zeros_like(wide)
    for c, target in enumerate(targets):
        wide[: geo.RP, :] = face[c]
        part = slice(c * geo.X, (c + 1) * geo.X)
        wide[pl.ds(0, geo.X, stride=geo.Y), :] = jnp.where(has_low, from_low[part, :], 0.0)
        wide[pl.ds(geo.sy + 1, geo.X, stride=geo.Y), :] = jnp.where(has_high, from_high[part, :], 0.0)
        target[0:8, :] = jnp.zeros((8, geo.LP), F32)
        target[geo.ZR - 8 : geo.ZR, :] = jnp.zeros((8, geo.LP), F32)
        target[2 : 2 + geo.sz, :] = wide[...].T
        target[1:2, :] = rows[c : c + 1]
        target[geo.sz + 2 : geo.sz + 3, :] = rows[16 + c : 17 + c]


def z_slab(geo, force, zbuf):
    zbuf[...] = jnp.zeros_like(zbuf)
    for c in range(3):
        zbuf[c, 0:2, :] = force[c, 1:3, :]
        zbuf[c, 2:4, :] = force[c, geo.sz + 1 : geo.sz + 3, :]


def sum_x_kernel(geo, flags, force, z_low, z_high, face, rows_out, x_low, x_high):
    has_low, has_high = flags[4] > 0, flags[5] > 0
    rows_out[...] = jnp.zeros_like(rows_out)
    x_low[...] = jnp.zeros_like(x_low)
    x_high[...] = jnp.zeros_like(x_high)
    span, two = geo.sx * geo.Y, 2 * geo.Y
    row = lax.broadcasted_iota(jnp.int32, (geo.sz, geo.LP), 0)
    for c in range(3):
        low = jnp.where(has_low, z_low[c, 2:4, :], 0.0)
        high = jnp.where(has_high, z_high[c, 0:2, :], 0.0)
        value = force[c, 2 : 2 + geo.sz, :]
        value = value + jnp.where(row == 0, low[1:2], 0.0)
        value = value + jnp.where(row == geo.sz - 1, high[0:1], 0.0)
        turned = value.T[: geo.RP]
        face[c] = turned
        low_row = force[c, 1:2, :] + low[0:1]
        high_row = force[c, geo.sz + 2 : geo.sz + 3, :] + high[1:2]
        rows_out[c : c + 1, :] = low_row
        rows_out[4 + c : 5 + c, :] = high_row
        x_low[c, 0:two, :] = face[c, 0:two, :]
        x_high[c, 0:two, :] = face[c, span : span + two, :]
        for buffer in (x_low, x_high):
            buffer[c, two : two + 1, :] = low_row
            buffer[c, two + 1 : two + 2, :] = high_row


def slab_rows(buffer, at):
    zero = jnp.zeros_like(buffer[0, at : at + 1, :])
    low = [buffer[c, at : at + 1, :] for c in range(3)]
    high = [buffer[c, at + 1 : at + 2, :] for c in range(3)]
    return jnp.concatenate(low + [zero] + high + [zero], 0)


def sum_y_kernel(geo, flags, face, rows_in, from_low, from_high, out, rows_out, y_low, y_high):
    has_low, has_high = flags[0] > 0, flags[1] > 0
    span, two = geo.sx * geo.Y, 2 * geo.Y
    rows = add_rows_x(
        geo, rows_in[...], slab_rows(from_low, two), slab_rows(from_high, two), has_low, has_high
    )
    rows_out[...] = rows
    out[...] = face[...]
    y_low[...] = jnp.zeros_like(y_low)
    y_high[...] = jnp.zeros_like(y_high)
    for c in range(3):
        out[c, 0:two, :] += jnp.where(has_low, from_low[c, 0:two, :], 0.0)
        out[c, span : span + two, :] += jnp.where(has_high, from_high[c, 0:two, :], 0.0)
        for plane in range(2):
            into = slice(plane * geo.X, (plane + 1) * geo.X)
            y_low[c, into, :] = out[c, pl.ds(plane, geo.X, stride=geo.Y), :]
            y_high[c, into, :] = out[c, pl.ds(geo.sy + plane, geo.X, stride=geo.Y), :]
        at = 2 * geo.X
        for buffer in (y_low, y_high):
            buffer[c, at : at + 1, :] = rows[c : c + 1]
            buffer[c, at + 1 : at + 2, :] = rows[4 + c : 5 + c]


def sum_done(geo, flags, face, rows_in, from_low, from_high, wide, total):
    has_low, has_high = flags[2] > 0, flags[3] > 0
    at = 2 * geo.X
    rows = add_rows_y(
        geo, rows_in[...], slab_rows(from_low, at), slab_rows(from_high, at), has_low, has_high
    )
    wide[...] = jnp.zeros_like(wide)
    for c in range(3):
        wide[: geo.RP, :] = face[c]
        for plane in range(2):
            part = slice(plane * geo.X, (plane + 1) * geo.X)
            low_at = pl.ds(plane, geo.X, stride=geo.Y)
            high_at = pl.ds(geo.sy + plane, geo.X, stride=geo.Y)
            wide[low_at, :] = wide[low_at, :] + jnp.where(has_low, from_low[c, part, :], 0.0)
            wide[high_at, :] = wide[high_at, :] + jnp.where(has_high, from_high[c, part, :], 0.0)
        total[c, 0:8, :] = jnp.zeros((8, geo.LP), F32)
        total[c, geo.ZR - 8 : geo.ZR, :] = jnp.zeros((8, geo.LP), F32)
        total[c, 2 : 2 + geo.sz, :] = wide[...].T
        total[c, 1:2, :] = rows[c : c + 1]
        total[c, geo.sz + 2 : geo.sz + 3, :] = rows[4 + c : 5 + c]


def update(geo, total, u, u_old, jinv, new_u, norm):
    lane, x, y = lane_xy(geo, (8, geo.LP))
    owned = (x >= 1) & (x <= geo.sx) & (y >= 1) & (y <= geo.sy)
    squares = jnp.zeros((8, geo.LP), F32)
    for k in range(geo.ZR // 8):
        rows = slice(8 * k, 8 * k + 8)
        now = [u[c, rows, :] for c in range(3)]
        residual = [now[c] - u_old[c, rows, :] - step_size * total[c, rows, :] for c in range(3)]
        for r in range(3):
            applied = sum(jinv[3 * r + m, rows, :] * residual[m] for m in range(3))
            new_u[r, rows, :] = now[r] - applied
        z = lax.broadcasted_iota(jnp.int32, (8, geo.LP), 0) + (8 * k - 1)
        mask = owned & (z >= 1) & (z <= geo.sz)
        square = residual[0] * residual[0] + residual[1] * residual[1] + residual[2] * residual[2]
        squares = squares + jnp.where(mask, square, 0.0)
    norm[...] = squares


def steps(code):
    which = code >> 1
    direction = 1 - 2 * (code & 1)
    return [jnp.where(which == k, direction, 0) for k in range(3)]


def split(value):
    high = value.astype(BF16).astype(F32)
    return high, value - high


def pair_pass(geo, base, u, codes, groups, both, work, frozen, force):
    windows, hots, gathered, sums = work
    LP, Y = geo.LP, geo.Y
    for k in range(geo.bz):
        window = u[:, 8 * k : 8 * k + 16, :].reshape(48, LP)
        high = window.astype(BF16)
        windows[k, :, :LP] = high
        windows[k, :, LP:] = (window - high.astype(F32)).astype(BF16)
    sums[...] = jnp.zeros_like(sums)
    lanes = lax.broadcasted_iota(jnp.int32, (LP, 512), 0)
    depths = lax.broadcasted_iota(jnp.int32, (16, 512), 0)

    def one_group(turn, carry):
        rows = pl.ds(pl.multiple_of(turn * GROUP, GROUP), GROUP)
        inside, along, offset, across = [codes[k, rows, :] for k in range(4)]
        kind = groups[rows, :]
        e1, e3 = steps(along), steps(across)
        third = (offset * 43) >> 7
        ninth = (offset * 57) >> 9
        shift = [ninth - 1, third - 3 * ninth - 1, offset - 3 * third - 1]
        lane_a = ((inside >> 5) + 1) * Y + ((inside >> 3) & 3) + 1
        depth_a = (inside & 7) + 2
        lane_b = lane_a + e1[0] * Y + e1[1]
        depth_b = depth_a + e1[2]
        lane_c = lane_a + shift[0] * Y + shift[1]
        depth_c = depth_a + shift[2]
        lane_d = lane_c + e3[0] * Y + e3[1]
        depth_d = depth_c + e3[2]
        lane4 = jnp.concatenate([lane_a, lane_b, lane_c, lane_d], 1)
        depth4 = jnp.concatenate([depth_a, depth_b, depth_c, depth_d], 1)
        places = []
        for t in range(GROUP):
            anchor = base[turn * GROUP + t]
            place = lax.rem(anchor, geo.bz)
            plane = lax.div(anchor, geo.bz)
            corner = 4 * Y * lax.div(plane, geo.by) + 4 * lax.rem(plane, geo.by)
            places.append(place)
            hot = jnp.where(lanes == lane4[t : t + 1] + corner, 1.0, 0.0).astype(BF16)
            hots[t] = hot
            picked = jnp.dot(
                windows[place], jnp.concatenate([hot, hot], 0), preferred_element_type=F32
            )
            mask = depths == depth4[t : t + 1]
            for c in range(3):
                part = jnp.where(mask, picked[16 * c : 16 * c + 16], 0.0)
                gathered[c, t : t + 1, :] = jnp.sum(part, 0, keepdims=True)
        line_one, line_two, apart = [], [], []
        for c in range(3):
            ua, ub, uc, ud = [gathered[c, :, 128 * n : 128 * n + 128] for n in range(4)]
            step1, step3 = e1[c].astype(F32), e3[c].astype(F32)
            line_one.append((ub - ua) + step1)
            line_two.append((ud - uc) + step3)
            lattice = shift[c].astype(F32) + 0.5 * (step3 - step1)
            apart.append(0.5 * ((uc + ud) - (ua + ub)) + lattice)
        square = apart[0] * apart[0] + apart[1] * apart[1] + apart[2] * apart[2] + core_square
        product = (
            line_one[0] * line_two[0] + line_one[1] * line_two[1] + line_one[2] * line_two[2]
        )
        coupling = (0.5 * stiffness) * product / (square * jnp.sqrt(square))
        pieces = []
        for group in (0, 1) if both else (0,):
            chosen = jnp.where(kind == group, coupling, 0.0)
            halves = [split(chosen * apart[c]) for c in range(3)]
            for piece in range(2):
                for c in range(3):
                    h = halves[c][piece]
                    pieces.append(jnp.concatenate([-h, -h, h, h], 1))
        for t in range(GROUP):
            mask = depths == depth4[t : t + 1]
            spread = jnp.concatenate(
                [jnp.where(mask, piece[t : t + 1], 0.0) for piece in pieces], 0
            ).astype(BF16)
            pushed = lax.dot_general(
                spread, hots[t], (((1,), (1,)), ((), ())), preferred_element_type=F32
            )
            for group in range(2 if both else 1):
                part = pushed[96 * group : 96 * group + 48] + pushed[96 * group + 48 : 96 * group + 96]
                sums[group, places[t]] += part
        return carry

    lax.fori_loop(0, geo.tiles // GROUP, one_group, 0)

    def folded(group, c, k):
        rows = jnp.zeros((8, LP), F32)
        if k < geo.bz:
            rows = rows + sums[group, k, 16 * c : 16 * c + 8, :]
        if k > 0:
            rows = rows + sums[group, k - 1, 16 * c + 8 : 16 * c + 16, :]
        return rows

    for c in range(3):
        for k in range(geo.bz + 1):
            rows = slice(8 * k, 8 * k + 8)
            if both:
                frozen[c, rows, :] = folded(1, c, k)
            force[c, rows, :] = folded(0, c, k) + frozen[c, rows, :]


def first_kernel(
    geo, base, flags, face, rows_in, from_low, from_high, codes, groups,
    u, u_old, jinv, frozen, force, zbuf, wide, *work,
):
    targets = [u.at[c] for c in range(3)] + [u_old.at[c] for c in range(3)]
    targets = targets + [jinv.at[c] for c in range(9)]
    fill_done(geo, flags, face, rows_in, from_low, from_high, wide, targets)
    pair_pass(geo, base, u, codes, groups, True, work, frozen, force)
    z_slab(geo, force, zbuf)


def next_kernel(
    geo, base, flags, face, rows_in, from_low, from_high, u, u_old, jinv, frozen, codes, groups,
    new_u, norm, force, zbuf, wide, total, *work,
):
    sum_done(geo, flags, face, rows_in, from_low, from_high, wide, total)
    update(geo, total, u, u_old, jinv, new_u, norm)
    pair_pass(geo, base, new_u, codes, groups, False, work, frozen, force)
    z_slab(geo, force, zbuf)


def last_kernel(
    geo, flags, face, rows_in, from_low, from_high, u, u_old, jinv, norm_0, norm_1,
    out, norms, wide, total, new_u, norm_2,
):
    sum_done(geo, flags, face, rows_in, from_low, from_high, wide, total)
    update(geo, total, u, u_old, jinv, new_u, norm_2)
    for c in range(3):
        wide[...] = new_u[c, 2 : 2 + geo.sz, :].T
        for x in range(geo.sx):
            start = (x + 1) * geo.Y + 1
            out[c, x * geo.sy : (x + 1) * geo.sy, :] = wide[start : start + geo.sy, :]
    lane = lax.broadcasted_iota(jnp.int32, (1, geo.LP), 1)
    line = jnp.zeros((1, geo.LP), F32)
    for k, norm in enumerate((norm_0, norm_1, norm_2)):
        line = line + jnp.where(lane == k, jnp.sum(norm[...]), 0.0)
    norms[...] = jnp.broadcast_to(line, norms.shape)


def ring(shard, axis, by):
    count = lax.axis_size(axis)
    return lax.ppermute(shard, axis, [(i, (i + by) % count) for i in range(count)])


def swap(low_buffer, high_buffer, axis):
    return ring(high_buffer, axis, 1), ring(low_buffer, axis, -1)


def swap_joint(buffer, axis):
    if lax.axis_size(axis) <= 2:
        other = ring(buffer, axis, 1)
        return other, other
    return ring(buffer, axis, 1), ring(buffer, axis, -1)


def per_device(u_old, u_trial, jacobian_inverse, tile_base, pair_codes, pair_groups):
    sx, sy, sz = u_old.shape[1:]
    geo = Geo(sx, sy, sz, tile_base.shape[0])
    if sz != 128 or geo.LP != 128 or sy % 8 or geo.tiles % GROUP:
        raise ValueError("unsupported sizes")
    axes = ("gx", "gy", "gz")
    cells = 3.0 * sx * sy * sz
    devices = 1
    limits = []
    for axis in axes:
        cells = cells * lax.axis_size(axis)
        devices = devices * lax.axis_size(axis)
        at = lax.axis_index(axis)
        limits += [(at > 0).astype(jnp.int32), (at < lax.axis_size(axis) - 1).astype(jnp.int32)]
    flags = jnp.stack(limits)
    vmem, smem = pl.BlockSpec(memory_space=pltpu.VMEM), pl.BlockSpec(memory_space=pltpu.SMEM)

    def arr(*shape):
        return jax.ShapeDtypeStruct(shape, F32)

    def call(kernel, name, scalars, operands, outs, scratch=()):
        return pl.pallas_call(
            functools.partial(kernel, geo),
            out_shape=outs,
            in_specs=[smem] * len(scalars) + [vmem] * len(operands),
            out_specs=[vmem] * len(outs),
            scratch_shapes=list(scratch),
            name=name,
        )(*scalars, *operands)

    def spot(*shape, dtype=F32):
        return pltpu.VMEM(shape, dtype)

    def work(count):
        return [
            spot(geo.bz, 48, 2 * geo.LP, dtype=BF16),
            spot(GROUP, geo.LP, 512, dtype=BF16),
            spot(3, GROUP, 512),
            spot(count, geo.bz, 48, geo.LP),
        ]

    square = spot(geo.LP, sz)
    lattice = arr(3, geo.ZR, geo.LP)
    faces3, rows8, zshape = arr(3, geo.RP, sz), arr(8, geo.LP), arr(3, 8, geo.LP)
    slab = arr(3, geo.slab, 128)

    ut = u_trial.reshape(3, sx * sy, sz)
    uo = u_old.reshape(3, sx * sy, sz)
    ji = jacobian_inverse.reshape(9, sx * sy, sz)

    face, zbuf = call(
        fill_z_kernel, "fill_z", [], [ut, uo, ji], [arr(15, geo.RP, sz), arr(32, geo.LP)], [square]
    )
    z_low, z_high = swap_joint(zbuf, "gz")
    wide_x = arr(15 * sy + 32, 128)
    x_low, x_high = call(
        fill_x_kernel, "fill_x", [flags], [ut, uo, ji, z_low, z_high], [wide_x, wide_x]
    )
    from_low, from_high = swap(x_low, x_high, "gx")
    wide_y = arr(fill_y_rows(geo), 128)
    face, rows, y_low, y_high = call(
        fill_y_kernel,
        "fill_y",
        [flags],
        [face, z_low, z_high, from_low, from_high],
        [arr(15, geo.RP, sz), arr(32, geo.LP), wide_y, wide_y],
    )
    from_low, from_high = swap(y_low, y_high, "gy")
    u, uo_l, ji_l, frozen, force, zbuf = call(
        first_kernel,
        "first_pass",
        [tile_base, flags],
        [face, rows, from_low, from_high, pair_codes, pair_groups],
        [lattice, lattice, arr(9, geo.ZR, geo.LP), lattice, lattice, zshape],
        [square] + work(2),
    )

    norm_list = []
    for iteration in range(ITERS):
        z_low, z_high = swap_joint(zbuf, "gz")
        face, rows, x_low, x_high = call(
            sum_x_kernel, "sum_x", [flags], [force, z_low, z_high], [faces3, rows8, slab, slab]
        )
        from_low, from_high = swap(x_low, x_high, "gx")
        face, rows, y_low, y_high = call(
            sum_y_kernel,
            "sum_y",
            [flags],
            [face, rows, from_low, from_high],
            [faces3, rows8, slab, slab],
        )
        from_low, from_high = swap(y_low, y_high, "gy")
        total = spot(3, geo.ZR, geo.LP)
        if iteration < ITERS - 1:
            u, norm, force, zbuf = call(
                next_kernel,
                "next_pass",
                [tile_base, flags],
                [face, rows, from_low, from_high, u, uo_l, ji_l, frozen, pair_codes, pair_groups],
                [lattice, rows8, lattice, zshape],
                [square, total] + work(1),
            )
            norm_list.append(norm)
    out, norms = call(
        last_kernel,
        "last",
        [flags],
        [face, rows, from_low, from_high, u, uo_l, ji_l] + norm_list,
        [arr(3, sx * sy, sz), arr(devices, 128)],
        [square, spot(3, geo.ZR, geo.LP), spot(3, geo.ZR, geo.LP), spot(8, geo.LP)],
    )
    spread = lax.all_to_all(norms.reshape(devices, 1, 128), axes, 0, 0)
    squares = jnp.sum(spread, axis=(0, 1))[:ITERS]
    return out.reshape(3, sx, sy, sz), jnp.sqrt(squares / cells)


def solution(mesh):
    return jax.shard_map(
        per_device,
        mesh=mesh,
        in_specs=(
            P(None, "gx", "gy", "gz"),
            P(None, "gx", "gy", "gz"),
            P(None, None, "gx", "gy", "gz"),
            P(("gx", "gy", "gz")),
            P(None, ("gx", "gy", "gz"), None),
            P(("gx", "gy", "gz"), None),
        ),
        out_specs=(P(None, "gx", "gy", "gz"), P()),
        check_vma=False,
    )
```

time: 1840 us -> 132 us (0.07); the launches traced: 1820 us -> 131 us
  local copies, waits for them, and re-layouts: 550 us -> 7.46 us
  other arithmetic: 515 us -> 1.09 us
  starting transfers between devices: 417 us -> 28.6 us
  blocking collectives: 172 us -> 13.2 us
  waiting for transfers between devices: 161 us -> 27.7 us
  Pallas kernels: 0 us -> 52.6 us
    gather x240 -> x0, local copies, waits for them, and re-layouts: 484 us -> none  [pair_terms(): points.append(lattice + flat_u[:, flat_fn(node_cell)])]
    scatter-add x36 -> x0, other arithmetic: 481 us -> none  [the longest x30 481 us: one_block(): summed.at[:, flat_index.reshape(-1)].add(values.reshape(channels, -1))]
    ppermute x36 -> x20, starting transfers between devices: 417 us -> 28.6 us  [ring(): lax.ppermute(shard, axis, [(i, (i + by) % count) for i in range(count)])]
    psum x1 -> x0, blocking collectives: 172 us -> none  [per_device(): squares_all = lax.psum(jnp.stack(square_list), ('gx', 'gy', 'gz'))]
    ppermute x36 -> x20, waiting for transfers between devices: 161 us -> 27.7 us  [ring(): lax.ppermute(shard, axis, [(i, (i + by) % count) for i in range(count)])]
    pallas_call x0 -> x13, Pallas kernels: none -> 52.6 us  [call(): pl.pallas_call(functools.partial(kernel, geo), out_shape=outs, in_specs=[...]
    while x6 -> x0, local copies, waits for them, and re-layouts: 26.3 us -> none  [accumulate(): summed = lax.fori_loop(0, block_turns, one_block, initial)]
  transfers between devices with their start and end apart: 36 -> 20, of which waited for: 25 -> 19; matrix products, arithmetic and copies ran while one was open for 0% -> 0% of each run, Pallas kernels for 0% -> 0%
where the time goes in v1:
time: 132 us; the launch traced here: 131 us
  Pallas kernels  52.6 us (40%)
  starting transfers between devices  28.6 us (22%)
  waiting for transfers between devices  27.7 us (21%)
  blocking collectives  13.2 us (10%)
  local copies, waits for them, and re-layouts  7.46 us (6%)
    pallas_call x13, Pallas kernels, call(): pl.pallas_call(functools.partial(kernel, geo), out_shape=outs, in_specs=[...  52.6 us
    ppermute x20, starting transfers between devices, ring(): lax.ppermute(shard, axis, [(i, (i + by) % count) for i in range(count)])  28.6 us
    ppermute x20, waiting for transfers between devices, ring(): lax.ppermute(shard, axis, [(i, (i + by) % count) for i in range(count)])  27.7 us
    all_to_all x1, blocking collectives, per_device(): spread = lax.all_to_all(norms.reshape(devices, 1, 128), axes, 0, 0)  13.2 us
    unnamed x40, local copies, waits for them, and re-layouts  7.35 us
  transfers between devices with their start and end apart: 20, of which 19 were waited for; matrix products, arithmetic and copies ran while one was open for 0% of the time, Pallas kernels for 0%

profile of v1, /device:TPU:0, one launch (start us, length us, event | category | flops | bytes accessed | tf_op | source)
XLA Modules:
  0.0 131.4 jit_solution(17692996117868519112)
XLA Ops:
  0.6 2.2 %fill_z.1 = (f32[15,104,128]{2,1,0:T(8,128)}, f32[32,128]{1,0:T(8,128)}) custom-call(f32[3,64,128]{2,1,0:T(8,128)} %bitcast.15, f32[3,64,128]{2,1,0:T(8,128)} %bitcast.17, f32[9,64,128]{2,1,0:T(8,128)} %bitcast.13), custom_call_target="tpu_custom_call" | custom-call | tf_op jit(solution)/shard_map/fill_z/pallas_call | solution.py:440
  2.9 0.5 collective-permute-start
  3.5 0.5 stack.36.flags
  4.0 0.4 collective-permute-done.z_low.z_high
  4.4 0.6 copy-done
  5.0 1.8 %fill_x.1 = (f32[152,128]{1,0:T(8,128)}, f32[152,128]{1,0:T(8,128)}) custom-call(s32[6]{0:T(128)} %stack.36.flags, f32[3,64,128]{2,1,0:T(8,128)} %bitcast.16, f32[3,64,128]{2,1,0:T(8,128)} %bitcast.18, f32[9,64,128]{2,1,0:T(8,128)} %bitcast.14, f32[32,128]{1,0:T(8,128)} %copy-done, f32[32,128]{1,0:T(8,128)} %copy-done), custom_call_target="tpu_custom_call" | custom-call | tf_op jit(solution)/shard_map/fill_x/pallas_call | solution.py:440
  6.8 2.9 %collective-permute-start.1 = (f32[152,128]{1,0:T(8,128)}, f32[152,128]{1,0:T(8,128)S(1)}, u32[]{:S(2)}, u32[]{:S(2)}) collective-permute-start(f32[152,128]{1,0:T(8,128)} %get-tuple-element.52), channel_id=1, source_target_pairs={{0,8},{8,16},{16,24},{24,0},{1,9},{9,17},{17,25},{25,1},{2,10},{10... | collective-permute-start | bytes 233480 | tf_op jit(solution)/shard_map/ppermute | solution.py:405
  9.7 2.0 %collective-permute-start.2 = (f32[152,128]{1,0:T(8,128)}, f32[152,128]{1,0:T(8,128)S(1)}, u32[]{:S(2)}, u32[]{:S(2)}) collective-permute-start(f32[152,128]{1,0:T(8,128)} %get-tuple-element.53), channel_id=1, source_target_pairs={{0,24},{8,0},{16,8},{24,16},{1,25},{9,1},{17,9},{25,17},{2,26},{10... | collective-permute-start | bytes 233480 | tf_op jit(solution)/shard_map/ppermute | solution.py:405
  11.7 3.1 %collective-permute-done.1.from_low = f32[152,128]{1,0:T(8,128)S(1)} collective-permute-done((f32[152,128]{1,0:T(8,128)}, f32[152,128]{1,0:T(8,128)S(1)}, u32[]{:S(2)}, u32[]{:S(2)}) %collective-permute-start.1) | collective-permute-done | bytes 77856 | tf_op jit(solution)/shard_map/ppermute | solution.py:405
  14.8 0.9 collective-permute-done.2.from_high
  15.7 0.6 copy-done.4
  16.3 2.2 %fill_y.1 = (f32[15,104,128]{2,1,0:T(8,128)}, f32[32,128]{1,0:T(8,128)}, f32[184,128]{1,0:T(8,128)}, f32[184,128]{1,0:T(8,128)}) custom-call(s32[6]{0:T(128)} %stack.36.flags, f32[15,104,128]{2,1,0:T(8,128)} %get-tuple-element.50.face, f32[32,128]{1,0:T(8,128)} %copy-done, f32[32,128]{1,0:T(8,128)} %copy-done, f32[152,128]{1,0:T(8,128)} %copy-done.3, ...), custom_call_target="tpu_custom_call" | custom-call | tf_op jit(solution)/shard_map/fill_y/pallas_call | solution.py:440
  18.5 1.5 %collective-permute-start.3 = (f32[184,128]{1,0:T(8,128)}, f32[184,128]{1,0:T(8,128)S(1)}, u32[]{:S(2)}, u32[]{:S(2)}) collective-permute-start(f32[184,128]{1,0:T(8,128)} %get-tuple-element.56), channel_id=1, source_target_pairs={{0,2},{2,4},{4,6},{6,0},{1,3},{3,5},{5,7},{7,1},{8,10},{10,12},{12... | collective-permute-start | bytes 282632 | tf_op jit(solution)/shard_map/ppermute | solution.py:405
  20.0 1.4 %collective-permute-start.4 = (f32[184,128]{1,0:T(8,128)}, f32[184,128]{1,0:T(8,128)S(1)}, u32[]{:S(2)}, u32[]{:S(2)}) collective-permute-start(f32[184,128]{1,0:T(8,128)} %get-tuple-element.57), channel_id=1, source_target_pairs={{0,6},{2,0},{4,2},{6,4},{1,7},{3,1},{5,3},{7,5},{8,14},{10,8},{12,... | collective-permute-start | bytes 282632 | tf_op jit(solution)/shard_map/ppermute | solution.py:405
  21.5 3.5 %collective-permute-done.3.from_low = f32[184,128]{1,0:T(8,128)S(1)} collective-permute-done((f32[184,128]{1,0:T(8,128)}, f32[184,128]{1,0:T(8,128)S(1)}, u32[]{:S(2)}, u32[]{:S(2)}) %collective-permute-start.3) | collective-permute-done | bytes 94240 | tf_op jit(solution)/shard_map/ppermute | solution.py:405
  25.0 0.8 collective-permute-done.4.from_high
  25.8 0.6 copy-done.2
  26.4 11.8 %first_pass.1 = (f32[3,136,128]{2,1,0:T(8,128)}, f32[3,136,128]{2,1,0:T(8,128)}, f32[9,136,128]{2,1,0:T(8,128)}, f32[3,136,128]{2,1,0:T(8,128)}, f32[3,136,128]{2,1,0:T(8,128)}, /*index=5*/f32[3,8,128]{2,1,0:T(8,128)}) custom-call(s32[64]{0:T(128)} %base.5, s32[6]{0:T(128)} %stack.36.flags, f32[15,104,128]{2,1,0:T(8,128)} %get-tuple-element.54.face, ...), custom_call_target="tpu_custom_call" | custom-call | tf_op jit(solution)/shard_map/first_pass/pallas_call | solution.py:440
  38.2 1.4 %collective-permute-done.5.z_low.z_high = f32[3,8,128]{2,1,0:T(8,128)S(1)} collective-permute-done((f32[3,8,128]{2,1,0:T(8,128)}, f32[3,8,128]{2,1,0:T(8,128)S(1)}, u32[]{:S(2)}, u32[]{:S(2)}) %collective-permute-start.5) | collective-permute-done | bytes 12320 | tf_op jit(solution)/shard_map/ppermute | solution.py:405
  39.6 0.6 copy-done.5
  40.2 1.8 %sum_x.3 = (f32[3,104,128]{2,1,0:T(8,128)}, f32[8,128]{1,0:T(8,128)}, f32[3,24,128]{2,1,0:T(8,128)}, f32[3,24,128]{2,1,0:T(8,128)}) custom-call(s32[6]{0:T(128)} %stack.36.flags, f32[3,136,128]{2,1,0:T(8,128)} %get-tuple-element.58.force, f32[3,8,128]{2,1,0:T(8,128)} %copy-done.5, f32[3,8,128]{2,1,0:T(8,128)} %copy-done.5), custom_call_target="tpu_custom_call" | custom-call | tf_op jit(solution)/shard_map/sum_x/pallas_call | solution.py:440
  42.0 1.7 %collective-permute-start.6 = (f32[3,24,128]{2,1,0:T(8,128)}, f32[3,24,128]{2,1,0:T(8,128)S(1)}, u32[]{:S(2)}, u32[]{:S(2)}) collective-permute-start(f32[3,24,128]{2,1,0:T(8,128)} %get-tuple-element.62), channel_id=1, source_target_pairs={{0,8},{8,16},{16,24},{24,0},{1,9},{9,17},{17,25},{25,1},{2,10},{10... | collective-permute-start | bytes 110600 | tf_op jit(solution)/shard_map/ppermute | solution.py:405
  43.6 2.1 %collective-permute-start.7 = (f32[3,24,128]{2,1,0:T(8,128)}, f32[3,24,128]{2,1,0:T(8,128)S(1)}, u32[]{:S(2)}, u32[]{:S(2)}) collective-permute-start(f32[3,24,128]{2,1,0:T(8,128)} %get-tuple-element.63), channel_id=1, source_target_pairs={{0,24},{8,0},{16,8},{24,16},{1,25},{9,1},{17,9},{25,17},{2,26},{10... | collective-permute-start | bytes 110600 | tf_op jit(solution)/shard_map/ppermute | solution.py:405
  45.8 2.2 %collective-permute-done.6.from_low = f32[3,24,128]{2,1,0:T(8,128)S(1)} collective-permute-done((f32[3,24,128]{2,1,0:T(8,128)}, f32[3,24,128]{2,1,0:T(8,128)S(1)}, u32[]{:S(2)}, u32[]{:S(2)}) %collective-permute-start.6) | collective-permute-done | bytes 36896 | tf_op jit(solution)/shard_map/ppermute | solution.py:405
  48.0 0.2 collective-permute-done.7.from_high
  48.2 0.4 copy-done.14
  48.6 0.2 copy-done.17
  48.8 1.7 %sum_y.3 = (f32[3,104,128]{2,1,0:T(8,128)}, f32[8,128]{1,0:T(8,128)}, f32[3,24,128]{2,1,0:T(8,128)}, f32[3,24,128]{2,1,0:T(8,128)}) custom-call(s32[6]{0:T(128)} %stack.36.flags, f32[3,104,128]{2,1,0:T(8,128)} %get-tuple-element.60.face, f32[8,128]{1,0:T(8,128)} %get-tuple-element.61.rows_in, f32[3,24,128]{2,1,0:T(8,128)} %copy-done.14, f32[3,24,128]{2,1,0:T(8,128)} %copy-done.17), custom_call_target="tpu_custom_call" | custom-call | tf_op jit(solution)/shard_map/sum_y/pallas_call | solution.py:440
  50.5 1.5 %collective-permute-start.8 = (f32[3,24,128]{2,1,0:T(8,128)}, f32[3,24,128]{2,1,0:T(8,128)S(1)}, u32[]{:S(2)}, u32[]{:S(2)}) collective-permute-start(f32[3,24,128]{2,1,0:T(8,128)} %get-tuple-element.66), channel_id=1, source_target_pairs={{0,2},{2,4},{4,6},{6,0},{1,3},{3,5},{5,7},{7,1},{8,10},{10,12},{12... | collective-permute-start | bytes 110600 | tf_op jit(solution)/shard_map/ppermute | solution.py:405
  52.0 1.4 %collective-permute-start.9 = (f32[3,24,128]{2,1,0:T(8,128)}, f32[3,24,128]{2,1,0:T(8,128)S(1)}, u32[]{:S(2)}, u32[]{:S(2)}) collective-permute-start(f32[3,24,128]{2,1,0:T(8,128)} %get-tuple-element.67), channel_id=1, source_target_pairs={{0,6},{2,0},{4,2},{6,4},{1,7},{3,1},{5,3},{7,5},{8,14},{10,8},{12,... | collective-permute-start | bytes 110600 | tf_op jit(solution)/shard_map/ppermute | solution.py:405
  53.4 2.1 %collective-permute-done.8.from_low = f32[3,24,128]{2,1,0:T(8,128)S(1)} collective-permute-done((f32[3,24,128]{2,1,0:T(8,128)}, f32[3,24,128]{2,1,0:T(8,128)S(1)}, u32[]{:S(2)}, u32[]{:S(2)}) %collective-permute-start.8) | collective-permute-done | bytes 36896 | tf_op jit(solution)/shard_map/ppermute | solution.py:405
  55.6 0.6 collective-permute-done.9.from_high
  56.2 0.6 copy-done.12
  56.8 11.0 %next_pass.2 = (f32[3,136,128]{2,1,0:T(8,128)}, f32[8,128]{1,0:T(8,128)}, f32[3,136,128]{2,1,0:T(8,128)}, f32[3,8,128]{2,1,0:T(8,128)}) custom-call(s32[64]{0:T(128)} %base.5, s32[6]{0:T(128)} %stack.36.flags, f32[3,104,128]{2,1,0:T(8,128)} %get-tuple-element.64.face, f32[8,128]{1,0:T(8,128)} %get-tuple-element.65.rows_in, f32[3,24,128]{2,1,0:T(8,128)} %copy-done.10, ...), custom_call_target="tpu_custom_call" | custom-call | tf_op jit(solution)/shard_map/next_pass/pallas_call | solution.py:440
  67.7 1.4 %collective-permute-done.10.z_low.z_high = f32[3,8,128]{2,1,0:T(8,128)S(1)} collective-permute-done((f32[3,8,128]{2,1,0:T(8,128)}, f32[3,8,128]{2,1,0:T(8,128)S(1)}, u32[]{:S(2)}, u32[]{:S(2)}) %collective-permute-start.10) | collective-permute-done | bytes 12320 | tf_op jit(solution)/shard_map/ppermute | solution.py:405
  69.1 0.6 copy-done.6
  69.7 1.8 %sum_x.4 = (f32[3,104,128]{2,1,0:T(8,128)}, f32[8,128]{1,0:T(8,128)}, f32[3,24,128]{2,1,0:T(8,128)}, f32[3,24,128]{2,1,0:T(8,128)}) custom-call(s32[6]{0:T(128)} %stack.36.flags, f32[3,136,128]{2,1,0:T(8,128)} %get-tuple-element.72.force, f32[3,8,128]{2,1,0:T(8,128)} %copy-done.6, f32[3,8,128]{2,1,0:T(8,128)} %copy-done.6), custom_call_target="tpu_custom_call" | custom-call | tf_op jit(solution)/shard_map/sum_x/pallas_call | solution.py:440
  71.5 3.8 %collective-permute-start.12 = (f32[3,24,128]{2,1,0:T(8,128)}, f32[3,24,128]{2,1,0:T(8,128)S(1)}, u32[]{:S(2)}, u32[]{:S(2)}) collective-permute-start(f32[3,24,128]{2,1,0:T(8,128)} %get-tuple-element.77), channel_id=1, source_target_pairs={{0,24},{8,0},{16,8},{24,16},{1,25},{9,1},{17,9},{25,17},{2,26},{10... | collective-permute-start | bytes 110600 | tf_op jit(solution)/shard_map/ppermute | solution.py:405
  75.3 2.1 %collective-permute-done.11.from_low = f32[3,24,128]{2,1,0:T(8,128)S(1)} collective-permute-done((f32[3,24,128]{2,1,0:T(8,128)}, f32[3,24,128]{2,1,0:T(8,128)S(1)}, u32[]{:S(2)}, u32[]{:S(2)}) %collective-permute-start.11) | collective-permute-done | bytes 36896 | tf_op jit(solution)/shard_map/ppermute | solution.py:405
  77.5 0.6 copy-done.15
  78.1 1.7 %sum_y.4 = (f32[3,104,128]{2,1,0:T(8,128)}, f32[8,128]{1,0:T(8,128)}, f32[3,24,128]{2,1,0:T(8,128)}, f32[3,24,128]{2,1,0:T(8,128)}) custom-call(s32[6]{0:T(128)} %stack.36.flags, f32[3,104,128]{2,1,0:T(8,128)} %get-tuple-element.74.face, f32[8,128]{1,0:T(8,128)} %get-tuple-element.75.rows_in, f32[3,24,128]{2,1,0:T(8,128)} %copy-done.15, f32[3,24,128]{2,1,0:T(8,128)} %copy-done.18), custom_call_target="tpu_custom_call" | custom-call | tf_op jit(solution)/shard_map/sum_y/pallas_call | solution.py:440
  79.8 1.4 %collective-permute-start.13 = (f32[3,24,128]{2,1,0:T(8,128)}, f32[3,24,128]{2,1,0:T(8,128)S(1)}, u32[]{:S(2)}, u32[]{:S(2)}) collective-permute-start(f32[3,24,128]{2,1,0:T(8,128)} %get-tuple-element.80), channel_id=1, source_target_pairs={{0,2},{2,4},{4,6},{6,0},{1,3},{3,5},{5,7},{7,1},{8,10},{10,12},{12... | collective-permute-start | bytes 110600 | tf_op jit(solution)/shard_map/ppermute | solution.py:405
  81.2 1.5 %collective-permute-start.14 = (f32[3,24,128]{2,1,0:T(8,128)}, f32[3,24,128]{2,1,0:T(8,128)S(1)}, u32[]{:S(2)}, u32[]{:S(2)}) collective-permute-start(f32[3,24,128]{2,1,0:T(8,128)} %get-tuple-element.81), channel_id=1, source_target_pairs={{0,6},{2,0},{4,2},{6,4},{1,7},{3,1},{5,3},{7,5},{8,14},{10,8},{12,... | collective-permute-start | bytes 110600 | tf_op jit(solution)/shard_map/ppermute | solution.py:405
  82.7 2.1 %collective-permute-done.13.from_low = f32[3,24,128]{2,1,0:T(8,128)S(1)} collective-permute-done((f32[3,24,128]{2,1,0:T(8,128)}, f32[3,24,128]{2,1,0:T(8,128)S(1)}, u32[]{:S(2)}, u32[]{:S(2)}) %collective-permute-start.13) | collective-permute-done | bytes 36896 | tf_op jit(solution)/shard_map/ppermute | solution.py:405
  84.8 0.5 collective-permute-done.14.from_high
  85.4 0.5 copy-done.13
  86.0 10.9 %next_pass.3 = (f32[3,136,128]{2,1,0:T(8,128)}, f32[8,128]{1,0:T(8,128)}, f32[3,136,128]{2,1,0:T(8,128)}, f32[3,8,128]{2,1,0:T(8,128)}) custom-call(s32[64]{0:T(128)} %base.5, s32[6]{0:T(128)} %stack.36.flags, f32[3,104,128]{2,1,0:T(8,128)} %get-tuple-element.78.face, f32[8,128]{1,0:T(8,128)} %get-tuple-element.79.rows_in, f32[3,24,128]{2,1,0:T(8,128)} %copy-done.11, ...), custom_call_target="tpu_custom_call" | custom-call | tf_op jit(solution)/shard_map/next_pass/pallas_call | solution.py:440
  96.9 1.4 %collective-permute-done.15.z_low.z_high = f32[3,8,128]{2,1,0:T(8,128)S(1)} collective-permute-done((f32[3,8,128]{2,1,0:T(8,128)}, f32[3,8,128]{2,1,0:T(8,128)S(1)}, u32[]{:S(2)}, u32[]{:S(2)}) %collective-permute-start.15) | collective-permute-done | bytes 12320 | tf_op jit(solution)/shard_map/ppermute | solution.py:405
  98.3 0.6 copy-done.7
  98.9 1.8 %sum_x.5 = (f32[3,104,128]{2,1,0:T(8,128)}, f32[8,128]{1,0:T(8,128)}, f32[3,24,128]{2,1,0:T(8,128)}, f32[3,24,128]{2,1,0:T(8,128)}) custom-call(s32[6]{0:T(128)} %stack.36.flags, f32[3,136,128]{2,1,0:T(8,128)} %get-tuple-element.83.force, f32[3,8,128]{2,1,0:T(8,128)} %copy-done.7, f32[3,8,128]{2,1,0:T(8,128)} %copy-done.7), custom_call_target="tpu_custom_call" | custom-call | tf_op jit(solution)/shard_map/sum_x/pallas_call | solution.py:440
  100.6 1.1 collective-permute-start.16
  101.8 2.8 %collective-permute-start.17 = (f32[3,24,128]{2,1,0:T(8,128)}, f32[3,24,128]{2,1,0:T(8,128)S(1)}, u32[]{:S(2)}, u32[]{:S(2)}) collective-permute-start(f32[3,24,128]{2,1,0:T(8,128)} %get-tuple-element.88), channel_id=1, source_target_pairs={{0,24},{8,0},{16,8},{24,16},{1,25},{9,1},{17,9},{25,17},{2,26},{10... | collective-permute-start | bytes 110600 | tf_op jit(solution)/shard_map/ppermute | solution.py:405
  104.5 2.1 %collective-permute-done.16.from_low = f32[3,24,128]{2,1,0:T(8,128)S(1)} collective-permute-done((f32[3,24,128]{2,1,0:T(8,128)}, f32[3,24,128]{2,1,0:T(8,128)S(1)}, u32[]{:S(2)}, u32[]{:S(2)}) %collective-permute-start.16) | collective-permute-done | bytes 36896 | tf_op jit(solution)/shard_map/ppermute | solution.py:405
  106.7 0.5 copy-done.16
  107.3 1.7 %sum_y.5 = (f32[3,104,128]{2,1,0:T(8,128)}, f32[8,128]{1,0:T(8,128)}, f32[3,24,128]{2,1,0:T(8,128)}, f32[3,24,128]{2,1,0:T(8,128)}) custom-call(s32[6]{0:T(128)} %stack.36.flags, f32[3,104,128]{2,1,0:T(8,128)} %get-tuple-element.85.face, f32[8,128]{1,0:T(8,128)} %get-tuple-element.86.rows_in, f32[3,24,128]{2,1,0:T(8,128)} %copy-done.16, f32[3,24,128]{2,1,0:T(8,128)} %copy-done.19), custom_call_target="tpu_custom_call" | custom-call | tf_op jit(solution)/shard_map/sum_y/pallas_call | solution.py:440
  109.0 1.4 %collective-permute-start.18 = (f32[3,24,128]{2,1,0:T(8,128)}, f32[3,24,128]{2,1,0:T(8,128)S(1)}, u32[]{:S(2)}, u32[]{:S(2)}) collective-permute-start(f32[3,24,128]{2,1,0:T(8,128)} %get-tuple-element.91), channel_id=1, source_target_pairs={{0,2},{2,4},{4,6},{6,0},{1,3},{3,5},{5,7},{7,1},{8,10},{10,12},{12... | collective-permute-start | bytes 110600 | tf_op jit(solution)/shard_map/ppermute | solution.py:405
  110.4 1.5 %collective-permute-start.19 = (f32[3,24,128]{2,1,0:T(8,128)}, f32[3,24,128]{2,1,0:T(8,128)S(1)}, u32[]{:S(2)}, u32[]{:S(2)}) collective-permute-start(f32[3,24,128]{2,1,0:T(8,128)} %get-tuple-element.92), channel_id=1, source_target_pairs={{0,6},{2,0},{4,2},{6,4},{1,7},{3,1},{5,3},{7,5},{8,14},{10,8},{12,... | collective-permute-start | bytes 110600 | tf_op jit(solution)/shard_map/ppermute | solution.py:405
  111.9 2.1 %collective-permute-done.18.from_low = f32[3,24,128]{2,1,0:T(8,128)S(1)} collective-permute-done((f32[3,24,128]{2,1,0:T(8,128)}, f32[3,24,128]{2,1,0:T(8,128)S(1)}, u32[]{:S(2)}, u32[]{:S(2)}) %collective-permute-start.18) | collective-permute-done | bytes 36896 | tf_op jit(solution)/shard_map/ppermute | solution.py:405
  114.1 0.5 collective-permute-done.19.from_high
  114.6 0.1 copy-done.8
  114.7 0.5 copy-done.9
  115.2 2.5 %last.1 = (f32[3,64,128]{2,1,0:T(8,128)}, f32[32,128]{1,0:T(8,128)}) custom-call(s32[6]{0:T(128)} %stack.36.flags, f32[3,104,128]{2,1,0:T(8,128)} %get-tuple-element.89.face, f32[8,128]{1,0:T(8,128)} %get-tuple-element.90.rows_in, f32[3,24,128]{2,1,0:T(8,128)} %copy-done.8, f32[3,24,128]{2,1,0:T(8,128)} %copy-done.9, f32[3,136,128]{2,1,0:T(8,128)} %get-tuple-element.93.u, ...), custom_call_target="tpu_custom_call" | custom-call | tf_op jit(solution)/shard_map/last/pallas_call | solution.py:440
  117.6 13.2 %all_to_all.5 = f32[32,1,128]{2,1,0:T(1,128)S(1)} all-to-all(f32[32,1,128]{2,1,0:T(1,128)} %bitcast.19), channel_id=1, replica_groups=mesh['gx'=4,'gy'=4,'gz'=2] {'gx','gy','gz'}, dimensions={0} | all-to-all | bytes 32768 | tf_op jit(solution)/shard_map/all_to_all | solution.py:530
  130.9 0.5 multiply_sqrt_fusion
  (34 shorter events, 0.5 us)
Async XLA Ops:
  2.9 1.5 %collective-permute-start = (f32[32,128]{1,0:T(8,128)}, f32[32,128]{1,0:T(8,128)S(1)}, u32[]{:S(2)}, u32[]{:S(2)}) collective-permute-start(f32[32,128]{1,0:T(8,128)} %get-tuple-element.51), channel_id=1, source_target_pairs={{0,1},{1,0},{2,3},{3,2},{4,5},{5,4},{6,7},{7,6},{8,9},{9,8},{10,11... | collective-permute-start | bytes 49160 | tf_op jit(solution)/shard_map/ppermute | solution.py:405
  4.4 0.6 copy-start
  6.8 8.0 %collective-permute-start.1 = (f32[152,128]{1,0:T(8,128)}, f32[152,128]{1,0:T(8,128)S(1)}, u32[]{:S(2)}, u32[]{:S(2)}) collective-permute-start(f32[152,128]{1,0:T(8,128)} %get-tuple-element.52), channel_id=1, source_target_pairs={{0,8},{8,16},{16,24},{24,0},{1,9},{9,17},{17,25},{25,1},{2,10},{10... | collective-permute-start | bytes 233480 | tf_op jit(solution)/shard_map/ppermute | solution.py:405
  9.7 6.0 %collective-permute-start.2 = (f32[152,128]{1,0:T(8,128)}, f32[152,128]{1,0:T(8,128)S(1)}, u32[]{:S(2)}, u32[]{:S(2)}) collective-permute-start(f32[152,128]{1,0:T(8,128)} %get-tuple-element.53), channel_id=1, source_target_pairs={{0,24},{8,0},{16,8},{24,16},{1,25},{9,1},{17,9},{25,17},{2,26},{10... | collective-permute-start | bytes 233480 | tf_op jit(solution)/shard_map/ppermute | solution.py:405
  14.8 0.9 copy-start.3
  15.7 0.6 copy-start.4
  18.5 6.4 %collective-permute-start.3 = (f32[184,128]{1,0:T(8,128)}, f32[184,128]{1,0:T(8,128)S(1)}, u32[]{:S(2)}, u32[]{:S(2)}) collective-permute-start(f32[184,128]{1,0:T(8,128)} %get-tuple-element.56), channel_id=1, source_target_pairs={{0,2},{2,4},{4,6},{6,0},{1,3},{3,5},{5,7},{7,1},{8,10},{10,12},{12... | collective-permute-start | bytes 282632 | tf_op jit(solution)/shard_map/ppermute | solution.py:405
  20.0 5.8 %collective-permute-start.4 = (f32[184,128]{1,0:T(8,128)}, f32[184,128]{1,0:T(8,128)S(1)}, u32[]{:S(2)}, u32[]{:S(2)}) collective-permute-start(f32[184,128]{1,0:T(8,128)} %get-tuple-element.57), channel_id=1, source_target_pairs={{0,6},{2,0},{4,2},{6,4},{1,7},{3,1},{5,3},{7,5},{8,14},{10,8},{12,... | collective-permute-start | bytes 282632 | tf_op jit(solution)/shard_map/ppermute | solution.py:405
  25.0 0.8 copy-start.1
  25.8 0.6 copy-start.2
  38.2 1.4 %collective-permute-start.5 = (f32[3,8,128]{2,1,0:T(8,128)}, f32[3,8,128]{2,1,0:T(8,128)S(1)}, u32[]{:S(2)}, u32[]{:S(2)}) collective-permute-start(f32[3,8,128]{2,1,0:T(8,128)} %get-tuple-element.59), channel_id=1, source_target_pairs={{0,1},{1,0},{2,3},{3,2},{4,5},{5,4},{6,7},{7,6},{8,9},{9,8},{10,11... | collective-permute-start | bytes 36872 | tf_op jit(solution)/shard_map/ppermute | solution.py:405
  39.6 0.6 copy-start.5
  42.0 6.1 %collective-permute-start.6 = (f32[3,24,128]{2,1,0:T(8,128)}, f32[3,24,128]{2,1,0:T(8,128)S(1)}, u32[]{:S(2)}, u32[]{:S(2)}) collective-permute-start(f32[3,24,128]{2,1,0:T(8,128)} %get-tuple-element.62), channel_id=1, source_target_pairs={{0,8},{8,16},{16,24},{24,0},{1,9},{9,17},{17,25},{25,1},{2,10},{10... | collective-permute-start | bytes 110600 | tf_op jit(solution)/shard_map/ppermute | solution.py:405
  43.6 4.6 %collective-permute-start.7 = (f32[3,24,128]{2,1,0:T(8,128)}, f32[3,24,128]{2,1,0:T(8,128)S(1)}, u32[]{:S(2)}, u32[]{:S(2)}) collective-permute-start(f32[3,24,128]{2,1,0:T(8,128)} %get-tuple-element.63), channel_id=1, source_target_pairs={{0,24},{8,0},{16,8},{24,16},{1,25},{9,1},{17,9},{25,17},{2,26},{10... | collective-permute-start | bytes 110600 | tf_op jit(solution)/shard_map/ppermute | solution.py:405
  48.0 0.6 copy-start.14
  48.2 0.6 copy-start.17
  50.5 5.1 %collective-permute-start.8 = (f32[3,24,128]{2,1,0:T(8,128)}, f32[3,24,128]{2,1,0:T(8,128)S(1)}, u32[]{:S(2)}, u32[]{:S(2)}) collective-permute-start(f32[3,24,128]{2,1,0:T(8,128)} %get-tuple-element.66), channel_id=1, source_target_pairs={{0,2},{2,4},{4,6},{6,0},{1,3},{3,5},{5,7},{7,1},{8,10},{10,12},{12... | collective-permute-start | bytes 110600 | tf_op jit(solution)/shard_map/ppermute | solution.py:405
  52.0 4.2 %collective-permute-start.9 = (f32[3,24,128]{2,1,0:T(8,128)}, f32[3,24,128]{2,1,0:T(8,128)S(1)}, u32[]{:S(2)}, u32[]{:S(2)}) collective-permute-start(f32[3,24,128]{2,1,0:T(8,128)} %get-tuple-element.67), channel_id=1, source_target_pairs={{0,6},{2,0},{4,2},{6,4},{1,7},{3,1},{5,3},{7,5},{8,14},{10,8},{12,... | collective-permute-start | bytes 110600 | tf_op jit(solution)/shard_map/ppermute | solution.py:405
  55.6 0.6 copy-start.10
  56.2 0.6 copy-start.12
  67.7 1.4 %collective-permute-start.10 = (f32[3,8,128]{2,1,0:T(8,128)}, f32[3,8,128]{2,1,0:T(8,128)S(1)}, u32[]{:S(2)}, u32[]{:S(2)}) collective-permute-start(f32[3,8,128]{2,1,0:T(8,128)} %get-tuple-element.73), channel_id=1, source_target_pairs={{0,1},{1,0},{2,3},{3,2},{4,5},{5,4},{6,7},{7,6},{8,9},{9,8},{10,11... | collective-permute-start | bytes 36872 | tf_op jit(solution)/shard_map/ppermute | solution.py:405
  69.1 0.6 copy-start.6
  71.5 6.0 %collective-permute-start.11 = (f32[3,24,128]{2,1,0:T(8,128)}, f32[3,24,128]{2,1,0:T(8,128)S(1)}, u32[]{:S(2)}, u32[]{:S(2)}) collective-permute-start(f32[3,24,128]{2,1,0:T(8,128)} %get-tuple-element.76), channel_id=1, source_target_pairs={{0,8},{8,16},{16,24},{24,0},{1,9},{9,17},{17,25},{25,1},{2,10},{10... | collective-permute-start | bytes 110600 | tf_op jit(solution)/shard_map/ppermute | solution.py:405
  71.5 6.0 %collective-permute-start.12 = (f32[3,24,128]{2,1,0:T(8,128)}, f32[3,24,128]{2,1,0:T(8,128)S(1)}, u32[]{:S(2)}, u32[]{:S(2)}) collective-permute-start(f32[3,24,128]{2,1,0:T(8,128)} %get-tuple-element.77), channel_id=1, source_target_pairs={{0,24},{8,0},{16,8},{24,16},{1,25},{9,1},{17,9},{25,17},{2,26},{10... | collective-permute-start | bytes 110600 | tf_op jit(solution)/shard_map/ppermute | solution.py:405
  77.5 0.6 copy-start.15
  77.5 0.6 copy-start.18
  79.8 5.1 %collective-permute-start.13 = (f32[3,24,128]{2,1,0:T(8,128)}, f32[3,24,128]{2,1,0:T(8,128)S(1)}, u32[]{:S(2)}, u32[]{:S(2)}) collective-permute-start(f32[3,24,128]{2,1,0:T(8,128)} %get-tuple-element.80), channel_id=1, source_target_pairs={{0,2},{2,4},{4,6},{6,0},{1,3},{3,5},{5,7},{7,1},{8,10},{10,12},{12... | collective-permute-start | bytes 110600 | tf_op jit(solution)/shard_map/ppermute | solution.py:405
  81.2 4.2 %collective-permute-start.14 = (f32[3,24,128]{2,1,0:T(8,128)}, f32[3,24,128]{2,1,0:T(8,128)S(1)}, u32[]{:S(2)}, u32[]{:S(2)}) collective-permute-start(f32[3,24,128]{2,1,0:T(8,128)} %get-tuple-element.81), channel_id=1, source_target_pairs={{0,6},{2,0},{4,2},{6,4},{1,7},{3,1},{5,3},{7,5},{8,14},{10,8},{12,... | collective-permute-start | bytes 110600 | tf_op jit(solution)/shard_map/ppermute | solution.py:405
  84.8 0.6 copy-start.11
  85.4 0.6 copy-start.13
  96.9 1.4 %collective-permute-start.15 = (f32[3,8,128]{2,1,0:T(8,128)}, f32[3,8,128]{2,1,0:T(8,128)S(1)}, u32[]{:S(2)}, u32[]{:S(2)}) collective-permute-start(f32[3,8,128]{2,1,0:T(8,128)} %get-tuple-element.84), channel_id=1, source_target_pairs={{0,1},{1,0},{2,3},{3,2},{4,5},{5,4},{6,7},{7,6},{8,9},{9,8},{10,11... | collective-permute-start | bytes 36872 | tf_op jit(solution)/shard_map/ppermute | solution.py:405
  98.3 0.6 copy-start.7
  100.6 6.0 %collective-permute-start.16 = (f32[3,24,128]{2,1,0:T(8,128)}, f32[3,24,128]{2,1,0:T(8,128)S(1)}, u32[]{:S(2)}, u32[]{:S(2)}) collective-permute-start(f32[3,24,128]{2,1,0:T(8,128)} %get-tuple-element.87), channel_id=1, source_target_pairs={{0,8},{8,16},{16,24},{24,0},{1,9},{9,17},{17,25},{25,1},{2,10},{10... | collective-permute-start | bytes 110600 | tf_op jit(solution)/shard_map/ppermute | solution.py:405
  101.8 5.0 %collective-permute-start.17 = (f32[3,24,128]{2,1,0:T(8,128)}, f32[3,24,128]{2,1,0:T(8,128)S(1)}, u32[]{:S(2)}, u32[]{:S(2)}) collective-permute-start(f32[3,24,128]{2,1,0:T(8,128)} %get-tuple-element.88), channel_id=1, source_target_pairs={{0,24},{8,0},{16,8},{24,16},{1,25},{9,1},{17,9},{25,17},{2,26},{10... | collective-permute-start | bytes 110600 | tf_op jit(solution)/shard_map/ppermute | solution.py:405
  106.6 0.6 copy-start.16
  106.7 0.6 copy-start.19
  109.0 5.1 %collective-permute-start.18 = (f32[3,24,128]{2,1,0:T(8,128)}, f32[3,24,128]{2,1,0:T(8,128)S(1)}, u32[]{:S(2)}, u32[]{:S(2)}) collective-permute-start(f32[3,24,128]{2,1,0:T(8,128)} %get-tuple-element.91), channel_id=1, source_target_pairs={{0,2},{2,4},{4,6},{6,0},{1,3},{3,5},{5,7},{7,1},{8,10},{10,12},{12... | collective-permute-start | bytes 110600 | tf_op jit(solution)/shard_map/ppermute | solution.py:405
  110.4 4.2 %collective-permute-start.19 = (f32[3,24,128]{2,1,0:T(8,128)}, f32[3,24,128]{2,1,0:T(8,128)S(1)}, u32[]{:S(2)}, u32[]{:S(2)}) collective-permute-start(f32[3,24,128]{2,1,0:T(8,128)} %get-tuple-element.92), channel_id=1, source_target_pairs={{0,6},{2,0},{4,2},{6,4},{1,7},{3,1},{5,3},{7,5},{8,14},{10,8},{12,... | collective-permute-start | bytes 110600 | tf_op jit(solution)/shard_map/ppermute | solution.py:405
  114.1 0.6 copy-start.8
  114.5 0.6 copy-start.9

commit v2 on v1

--- a/solution.py
+++ b/solution.py
@@ -15,6 +15,7 @@
 F32 = jnp.float32
 BF16 = jnp.bfloat16
 GROUP = 8
+VMEM_GRANT = 12 << 20
 
 
 class Geo:
@@ -443,6 +444,7 @@
             in_specs=[smem] * len(scalars) + [vmem] * len(operands),
             out_specs=[vmem] * len(outs),
             scratch_shapes=list(scratch),
+            compiler_params=pltpu.CompilerParams(vmem_limit_bytes=VMEM_GRANT),
             name=name,
         )(*scalars, *operands)
 

time: 132 us -> 109 us (0.83)
  Pallas kernels: 52.6 us -> 36 us
  local copies, waits for them, and re-layouts: 7.46 us -> 3.51 us
  waiting for transfers between devices: 27.7 us -> 25.6 us
    pallas_call x13, Pallas kernels: 52.6 us -> 36 us  [call(): pl.pallas_call(functools.partial(kernel, geo), out_shape=outs, in_specs=[...]
    unnamed x40 -> x18, local copies, waits for them, and re-layouts: 7.35 us -> 3.41 us
    ppermute x20, waiting for transfers between devices: 27.7 us -> 25.6 us  [ring(): lax.ppermute(shard, axis, [(i, (i + by) % count) for i in range(count)])]
where the time goes in v2:
time: 109 us
  Pallas kernels  36 us (33%)
  starting transfers between devices  29.4 us (27%)
  waiting for transfers between devices  25.6 us (23%)
  blocking collectives  13 us (12%)
  local copies, waits for them, and re-layouts  3.51 us (3%)
    pallas_call x13, Pallas kernels, call(): pl.pallas_call(functools.partial(kernel, geo), out_shape=outs, in_specs=[...  36 us
    ppermute x20, starting transfers between devices, ring(): lax.ppermute(shard, axis, [(i, (i + by) % count) for i in range(count)])  29.4 us
    ppermute x20, waiting for transfers between devices, ring(): lax.ppermute(shard, axis, [(i, (i + by) % count) for i in range(count)])  25.6 us
    all_to_all x1, blocking collectives, per_device(): spread = lax.all_to_all(norms.reshape(devices, 1, 128), axes, 0, 0)  13 us
    unnamed x18, local copies, waits for them, and re-layouts  3.41 us
  transfers between devices with their start and end apart: 20, of which 19 were waited for; matrix products, arithmetic and copies ran while one was open for 0% of the time, Pallas kernels for 0%

profile of v2, /device:TPU:0, one launch (start us, length us, event | category | flops | bytes accessed | tf_op | source)
XLA Modules:
  0.0 108.8 jit_solution(3249493616979926156)
XLA Ops:
  0.6 0.0 copy-start
  0.6 1.0 copy-done
  1.6 0.9 copy-done.3
  2.5 0.9 copy-done.5
  3.4 0.4 fill_z.1
  3.8 0.6 collective-permute-start
  4.3 0.1 stack.35
  4.4 0.7 collective-permute-done.z_low.z_high
  5.2 0.0 copy-done.4
  5.2 0.6 fill_x.1
  5.7 3.0 %collective-permute-start.1 = (f32[152,128]{1,0:T(8,128)S(1)}, f32[152,128]{1,0:T(8,128)S(1)}, u32[]{:S(2)}, u32[]{:S(2)}) collective-permute-start(f32[152,128]{1,0:T(8,128)S(1)} %get-tuple-element.52), channel_id=1, source_target_pairs={{0,8},{8,16},{16,24},{24,0},{1,9},{9,17},{17,25},{25,1},{2,10},{10... | collective-permute-start | bytes 233480 | tf_op jit(solution)/shard_map/ppermute | solution.py:406
  8.7 2.1 %collective-permute-start.2 = (f32[152,128]{1,0:T(8,128)S(1)}, f32[152,128]{1,0:T(8,128)S(1)}, u32[]{:S(2)}, u32[]{:S(2)}) collective-permute-start(f32[152,128]{1,0:T(8,128)S(1)} %get-tuple-element.53), channel_id=1, source_target_pairs={{0,24},{8,0},{16,8},{24,16},{1,25},{9,1},{17,9},{25,17},{2,26},{10... | collective-permute-start | bytes 233480 | tf_op jit(solution)/shard_map/ppermute | solution.py:406
  10.8 2.8 %collective-permute-done.1.from_low = f32[152,128]{1,0:T(8,128)S(1)} collective-permute-done((f32[152,128]{1,0:T(8,128)S(1)}, f32[152,128]{1,0:T(8,128)S(1)}, u32[]{:S(2)}, u32[]{:S(2)}) %collective-permute-start.1) | collective-permute-done | bytes 77856 | tf_op jit(solution)/shard_map/ppermute | solution.py:406
  13.6 0.9 collective-permute-done.2.from_high
  14.5 0.6 fill_y.1
  15.2 1.5 %collective-permute-start.3 = (f32[184,128]{1,0:T(8,128)S(1)}, f32[184,128]{1,0:T(8,128)S(1)}, u32[]{:S(2)}, u32[]{:S(2)}) collective-permute-start(f32[184,128]{1,0:T(8,128)S(1)} %get-tuple-element.56), channel_id=1, source_target_pairs={{0,2},{2,4},{4,6},{6,0},{1,3},{3,5},{5,7},{7,1},{8,10},{10,12},{12... | collective-permute-start | bytes 282632 | tf_op jit(solution)/shard_map/ppermute | solution.py:406
  16.7 1.4 %collective-permute-start.4 = (f32[184,128]{1,0:T(8,128)S(1)}, f32[184,128]{1,0:T(8,128)S(1)}, u32[]{:S(2)}, u32[]{:S(2)}) collective-permute-start(f32[184,128]{1,0:T(8,128)S(1)} %get-tuple-element.57), channel_id=1, source_target_pairs={{0,6},{2,0},{4,2},{6,4},{1,7},{3,1},{5,3},{7,5},{8,14},{10,8},{12,... | collective-permute-start | bytes 282632 | tf_op jit(solution)/shard_map/ppermute | solution.py:406
  18.1 3.3 %collective-permute-done.3.from_low = f32[184,128]{1,0:T(8,128)S(1)} collective-permute-done((f32[184,128]{1,0:T(8,128)S(1)}, f32[184,128]{1,0:T(8,128)S(1)}, u32[]{:S(2)}, u32[]{:S(2)}) %collective-permute-start.3) | collective-permute-done | bytes 94240 | tf_op jit(solution)/shard_map/ppermute | solution.py:406
  21.4 0.8 collective-permute-done.4.from_high
  22.2 0.0 copy-done.7
  22.2 0.6 copy-done.8
  22.9 10.3 %first_pass.1 = (f32[3,136,128]{2,1,0:T(8,128)S(1)}, f32[3,136,128]{2,1,0:T(8,128)S(1)}, f32[9,136,128]{2,1,0:T(8,128)S(1)}, f32[3,136,128]{2,1,0:T(8,128)S(1)},...) custom-call(s32[64]{0:T(128)S(1)} %copy-done.8, s32[6]{0:T(128)S(1)} %stack.36.flags, ...), custom_call_target="tpu_custom_call" | custom-call | tf_op jit(solution)/shard_map/first_pass/pallas_call | solution.py:441
  33.3 0.1 collective-permute-start.5
  33.3 1.2 %collective-permute-done.5.z_low.z_high = f32[3,8,128]{2,1,0:T(8,128)S(1)} collective-permute-done((f32[3,8,128]{2,1,0:T(8,128)S(1)}, f32[3,8,128]{2,1,0:T(8,128)S(1)}, u32[]{:S(2)}, u32[]{:S(2)}) %collective-permute-start.5) | collective-permute-done | bytes 12320 | tf_op jit(solution)/shard_map/ppermute | solution.py:406
  34.5 0.7 sum_x.3
  35.2 1.7 %collective-permute-start.6 = (f32[3,24,128]{2,1,0:T(8,128)S(1)}, f32[3,24,128]{2,1,0:T(8,128)S(1)}, u32[]{:S(2)}, u32[]{:S(2)}) collective-permute-start(f32[3,24,128]{2,1,0:T(8,128)S(1)} %get-tuple-element.62), channel_id=1, source_target_pairs={{0,8},{8,16},{16,24},{24,0},{1,9},{9,17},{17,25},{25,1},{2,10},{10... | collective-permute-start | bytes 110600 | tf_op jit(solution)/shard_map/ppermute | solution.py:406
  36.9 2.1 %collective-permute-start.7 = (f32[3,24,128]{2,1,0:T(8,128)S(1)}, f32[3,24,128]{2,1,0:T(8,128)S(1)}, u32[]{:S(2)}, u32[]{:S(2)}) collective-permute-start(f32[3,24,128]{2,1,0:T(8,128)S(1)} %get-tuple-element.63), channel_id=1, source_target_pairs={{0,24},{8,0},{16,8},{24,16},{1,25},{9,1},{17,9},{25,17},{2,26},{10... | collective-permute-start | bytes 110600 | tf_op jit(solution)/shard_map/ppermute | solution.py:406
  39.0 1.9 %collective-permute-done.6.from_low = f32[3,24,128]{2,1,0:T(8,128)S(1)} collective-permute-done((f32[3,24,128]{2,1,0:T(8,128)S(1)}, f32[3,24,128]{2,1,0:T(8,128)S(1)}, u32[]{:S(2)}, u32[]{:S(2)}) %collective-permute-start.6) | collective-permute-done | bytes 36896 | tf_op jit(solution)/shard_map/ppermute | solution.py:406
  41.0 0.3 collective-permute-done.7.from_high
  41.3 0.6 sum_y.3
  41.9 1.5 %collective-permute-start.8 = (f32[3,24,128]{2,1,0:T(8,128)S(1)}, f32[3,24,128]{2,1,0:T(8,128)S(1)}, u32[]{:S(2)}, u32[]{:S(2)}) collective-permute-start(f32[3,24,128]{2,1,0:T(8,128)S(1)} %get-tuple-element.66), channel_id=1, source_target_pairs={{0,2},{2,4},{4,6},{6,0},{1,3},{3,5},{5,7},{7,1},{8,10},{10,12},{12... | collective-permute-start | bytes 110600 | tf_op jit(solution)/shard_map/ppermute | solution.py:406
  43.4 1.4 %collective-permute-start.9 = (f32[3,24,128]{2,1,0:T(8,128)S(1)}, f32[3,24,128]{2,1,0:T(8,128)S(1)}, u32[]{:S(2)}, u32[]{:S(2)}) collective-permute-start(f32[3,24,128]{2,1,0:T(8,128)S(1)} %get-tuple-element.67), channel_id=1, source_target_pairs={{0,6},{2,0},{4,2},{6,4},{1,7},{3,1},{5,3},{7,5},{8,14},{10,8},{12,... | collective-permute-start | bytes 110600 | tf_op jit(solution)/shard_map/ppermute | solution.py:406
  44.8 1.9 %collective-permute-done.8.from_low = f32[3,24,128]{2,1,0:T(8,128)S(1)} collective-permute-done((f32[3,24,128]{2,1,0:T(8,128)S(1)}, f32[3,24,128]{2,1,0:T(8,128)S(1)}, u32[]{:S(2)}, u32[]{:S(2)}) %collective-permute-start.8) | collective-permute-done | bytes 36896 | tf_op jit(solution)/shard_map/ppermute | solution.py:406
  46.8 0.6 collective-permute-done.9.from_high
  47.4 9.3 %next_pass.2 = (f32[3,136,128]{2,1,0:T(8,128)S(1)}, f32[8,128]{1,0:T(8,128)S(1)}, f32[3,136,128]{2,1,0:T(8,128)S(1)}, f32[3,8,128]{2,1,0:T(8,128)S(1)}) custom-call(s32[64]{0:T(128)S(1)} %copy-done.8, s32[6]{0:T(128)S(1)} %stack.36.flags, f32[3,104,128]{2,1,0:T(8,128)S(1)} %get-tuple-element.64.face, f32[8,128]{1,0:T(8,128)S(1)} %get-tuple-element.65.rows_in, ...), custom_call_target="tpu_custom_call" | custom-call | tf_op jit(solution)/shard_map/next_pass/pallas_call | solution.py:441
  56.7 0.1 collective-permute-start.10
  56.8 1.2 %collective-permute-done.10.z_low.z_high = f32[3,8,128]{2,1,0:T(8,128)S(1)} collective-permute-done((f32[3,8,128]{2,1,0:T(8,128)S(1)}, f32[3,8,128]{2,1,0:T(8,128)S(1)}, u32[]{:S(2)}, u32[]{:S(2)}) %collective-permute-start.10) | collective-permute-done | bytes 12320 | tf_op jit(solution)/shard_map/ppermute | solution.py:406
  57.9 0.7 sum_x.4
  58.6 0.1 collective-permute-start.11
  58.7 3.8 %collective-permute-start.12 = (f32[3,24,128]{2,1,0:T(8,128)S(1)}, f32[3,24,128]{2,1,0:T(8,128)S(1)}, u32[]{:S(2)}, u32[]{:S(2)}) collective-permute-start(f32[3,24,128]{2,1,0:T(8,128)S(1)} %get-tuple-element.77), channel_id=1, source_target_pairs={{0,24},{8,0},{16,8},{24,16},{1,25},{9,1},{17,9},{25,17},{2,26},{10... | collective-permute-start | bytes 110600 | tf_op jit(solution)/shard_map/ppermute | solution.py:406
  62.5 1.9 %collective-permute-done.11.from_low = f32[3,24,128]{2,1,0:T(8,128)S(1)} collective-permute-done((f32[3,24,128]{2,1,0:T(8,128)S(1)}, f32[3,24,128]{2,1,0:T(8,128)S(1)}, u32[]{:S(2)}, u32[]{:S(2)}) %collective-permute-start.11) | collective-permute-done | bytes 36896 | tf_op jit(solution)/shard_map/ppermute | solution.py:406
  64.4 0.0 collective-permute-done.12.from_high
  64.4 0.6 sum_y.4
  65.0 1.5 %collective-permute-start.13 = (f32[3,24,128]{2,1,0:T(8,128)S(1)}, f32[3,24,128]{2,1,0:T(8,128)S(1)}, u32[]{:S(2)}, u32[]{:S(2)}) collective-permute-start(f32[3,24,128]{2,1,0:T(8,128)S(1)} %get-tuple-element.80), channel_id=1, source_target_pairs={{0,2},{2,4},{4,6},{6,0},{1,3},{3,5},{5,7},{7,1},{8,10},{10,12},{12... | collective-permute-start | bytes 110600 | tf_op jit(solution)/shard_map/ppermute | solution.py:406
  66.5 1.5 %collective-permute-start.14 = (f32[3,24,128]{2,1,0:T(8,128)S(1)}, f32[3,24,128]{2,1,0:T(8,128)S(1)}, u32[]{:S(2)}, u32[]{:S(2)}) collective-permute-start(f32[3,24,128]{2,1,0:T(8,128)S(1)} %get-tuple-element.81), channel_id=1, source_target_pairs={{0,6},{2,0},{4,2},{6,4},{1,7},{3,1},{5,3},{7,5},{8,14},{10,8},{12,... | collective-permute-start | bytes 110600 | tf_op jit(solution)/shard_map/ppermute | solution.py:406
  68.0 1.9 %collective-permute-done.13.from_low = f32[3,24,128]{2,1,0:T(8,128)S(1)} collective-permute-done((f32[3,24,128]{2,1,0:T(8,128)S(1)}, f32[3,24,128]{2,1,0:T(8,128)S(1)}, u32[]{:S(2)}, u32[]{:S(2)}) %collective-permute-start.13) | collective-permute-done | bytes 36896 | tf_op jit(solution)/shard_map/ppermute | solution.py:406
  69.9 0.5 collective-permute-done.14.from_high
  70.5 9.3 %next_pass.3 = (f32[3,136,128]{2,1,0:T(8,128)S(1)}, f32[8,128]{1,0:T(8,128)S(1)}, f32[3,136,128]{2,1,0:T(8,128)S(1)}, f32[3,8,128]{2,1,0:T(8,128)S(1)}) custom-call(s32[64]{0:T(128)S(1)} %copy-done.8, s32[6]{0:T(128)S(1)} %stack.36.flags, f32[3,104,128]{2,1,0:T(8,128)S(1)} %get-tuple-element.78.face, f32[8,128]{1,0:T(8,128)S(1)} %get-tuple-element.79.rows_in, ...), custom_call_target="tpu_custom_call" | custom-call | tf_op jit(solution)/shard_map/next_pass/pallas_call | solution.py:441
  79.8 0.1 collective-permute-start.15
  79.8 1.2 %collective-permute-done.15.z_low.z_high = f32[3,8,128]{2,1,0:T(8,128)S(1)} collective-permute-done((f32[3,8,128]{2,1,0:T(8,128)S(1)}, f32[3,8,128]{2,1,0:T(8,128)S(1)}, u32[]{:S(2)}, u32[]{:S(2)}) %collective-permute-start.15) | collective-permute-done | bytes 12320 | tf_op jit(solution)/shard_map/ppermute | solution.py:406
  81.0 0.7 sum_x.5
  81.7 1.2 %collective-permute-start.16 = (f32[3,24,128]{2,1,0:T(8,128)S(1)}, f32[3,24,128]{2,1,0:T(8,128)S(1)}, u32[]{:S(2)}, u32[]{:S(2)}) collective-permute-start(f32[3,24,128]{2,1,0:T(8,128)S(1)} %get-tuple-element.87), channel_id=1, source_target_pairs={{0,8},{8,16},{16,24},{24,0},{1,9},{9,17},{17,25},{25,1},{2,10},{10... | collective-permute-start | bytes 110600 | tf_op jit(solution)/shard_map/ppermute | solution.py:406
  82.9 2.7 %collective-permute-start.17 = (f32[3,24,128]{2,1,0:T(8,128)S(1)}, f32[3,24,128]{2,1,0:T(8,128)S(1)}, u32[]{:S(2)}, u32[]{:S(2)}) collective-permute-start(f32[3,24,128]{2,1,0:T(8,128)S(1)} %get-tuple-element.88), channel_id=1, source_target_pairs={{0,24},{8,0},{16,8},{24,16},{1,25},{9,1},{17,9},{25,17},{2,26},{10... | collective-permute-start | bytes 110600 | tf_op jit(solution)/shard_map/ppermute | solution.py:406
  85.6 1.9 %collective-permute-done.16.from_low = f32[3,24,128]{2,1,0:T(8,128)S(1)} collective-permute-done((f32[3,24,128]{2,1,0:T(8,128)S(1)}, f32[3,24,128]{2,1,0:T(8,128)S(1)}, u32[]{:S(2)}, u32[]{:S(2)}) %collective-permute-start.16) | collective-permute-done | bytes 36896 | tf_op jit(solution)/shard_map/ppermute | solution.py:406
  87.5 0.1 collective-permute-done.17.from_high
  87.6 0.6 sum_y.5
  88.3 1.4 %collective-permute-start.18 = (f32[3,24,128]{2,1,0:T(8,128)S(1)}, f32[3,24,128]{2,1,0:T(8,128)S(1)}, u32[]{:S(2)}, u32[]{:S(2)}) collective-permute-start(f32[3,24,128]{2,1,0:T(8,128)S(1)} %get-tuple-element.91), channel_id=1, source_target_pairs={{0,2},{2,4},{4,6},{6,0},{1,3},{3,5},{5,7},{7,1},{8,10},{10,12},{12... | collective-permute-start | bytes 110600 | tf_op jit(solution)/shard_map/ppermute | solution.py:406
  89.6 1.6 %collective-permute-start.19 = (f32[3,24,128]{2,1,0:T(8,128)S(1)}, f32[3,24,128]{2,1,0:T(8,128)S(1)}, u32[]{:S(2)}, u32[]{:S(2)}) collective-permute-start(f32[3,24,128]{2,1,0:T(8,128)S(1)} %get-tuple-element.92), channel_id=1, source_target_pairs={{0,6},{2,0},{4,2},{6,4},{1,7},{3,1},{5,3},{7,5},{8,14},{10,8},{12,... | collective-permute-start | bytes 110600 | tf_op jit(solution)/shard_map/ppermute | solution.py:406
  91.2 1.9 %collective-permute-done.18.from_low = f32[3,24,128]{2,1,0:T(8,128)S(1)} collective-permute-done((f32[3,24,128]{2,1,0:T(8,128)S(1)}, f32[3,24,128]{2,1,0:T(8,128)S(1)}, u32[]{:S(2)}, u32[]{:S(2)}) %collective-permute-start.18) | collective-permute-done | bytes 36896 | tf_op jit(solution)/shard_map/ppermute | solution.py:406
  93.1 0.5 collective-permute-done.19.from_high
  93.6 1.6 %last.1 = (f32[3,64,128]{2,1,0:T(8,128)}, f32[32,128]{1,0:T(8,128)S(1)}) custom-call(s32[6]{0:T(128)S(1)} %stack.36.flags, f32[3,104,128]{2,1,0:T(8,128)S(1)} %get-tuple-element.89.face, f32[8,128]{1,0:T(8,128)S(1)} %get-tuple-element.90.rows_in, f32[3,24,128]{2,1,0:T(8,128)S(1)} %collective-permute-done.18.from_low, ...), custom_call_target="tpu_custom_call" | custom-call | tf_op jit(solution)/shard_map/last/pallas_call | solution.py:441
  95.2 13.0 %all_to_all.5 = f32[32,1,128]{2,1,0:T(1,128)S(1)} all-to-all(f32[32,1,128]{2,1,0:T(1,128)S(1)} %bitcast.19), channel_id=1, replica_groups=mesh['gx'=4,'gy'=4,'gz'=2] {'gx','gy','gz'}, dimensions={0} | all-to-all | bytes 32768 | tf_op jit(solution)/shard_map/all_to_all | solution.py:532
  108.2 0.1 reduce_sum.9
  108.3 0.5 multiply_sqrt_fusion
  (12 shorter events, 0.0 us)
Async XLA Ops:
  0.6 1.0 copy-start
  1.6 0.9 copy-start.3
  2.5 0.9 copy-start.5
  3.4 1.8 %copy-start.1 = (f32[3,3,8,8,128]{4,3,2,1,0:T(8,128)S(1)}, f32[3,3,8,8,128]{4,3,2,1,0:T(8,128)}, u32[]{:S(2)}) copy-start(f32[3,3,8,8,128]{4,3,2,1,0:T(8,128)} %param.8) | copy-start | bytes 884740
  3.4 1.8 %copy-start.4 = (f32[3,8,8,128]{3,2,1,0:T(8,128)S(1)}, f32[3,8,8,128]{3,2,1,0:T(8,128)}, u32[]{:S(2)}) copy-start(f32[3,8,8,128]{3,2,1,0:T(8,128)} %param.7) | copy-start | bytes 294916
  3.4 1.8 %copy-start.6 = (f32[3,8,8,128]{3,2,1,0:T(8,128)S(1)}, f32[3,8,8,128]{3,2,1,0:T(8,128)}, u32[]{:S(2)}) copy-start(f32[3,8,8,128]{3,2,1,0:T(8,128)} %param.6) | copy-start | bytes 294916
  3.8 1.4 %collective-permute-start = (f32[32,128]{1,0:T(8,128)S(1)}, f32[32,128]{1,0:T(8,128)S(1)}, u32[]{:S(2)}, u32[]{:S(2)}) collective-permute-start(f32[32,128]{1,0:T(8,128)S(1)} %get-tuple-element.51), channel_id=1, source_target_pairs={{0,1},{1,0},{2,3},{3,2},{4,5},{5,4},{6,7},{7,6},{8,9},{9,8},{10,11... | collective-permute-start | bytes 49160 | tf_op jit(solution)/shard_map/ppermute | solution.py:406
  5.7 7.9 %collective-permute-start.1 = (f32[152,128]{1,0:T(8,128)S(1)}, f32[152,128]{1,0:T(8,128)S(1)}, u32[]{:S(2)}, u32[]{:S(2)}) collective-permute-start(f32[152,128]{1,0:T(8,128)S(1)} %get-tuple-element.52), channel_id=1, source_target_pairs={{0,8},{8,16},{16,24},{24,0},{1,9},{9,17},{17,25},{25,1},{2,10},{10... | collective-permute-start | bytes 233480 | tf_op jit(solution)/shard_map/ppermute | solution.py:406
  8.7 5.8 %collective-permute-start.2 = (f32[152,128]{1,0:T(8,128)S(1)}, f32[152,128]{1,0:T(8,128)S(1)}, u32[]{:S(2)}, u32[]{:S(2)}) collective-permute-start(f32[152,128]{1,0:T(8,128)S(1)} %get-tuple-element.53), channel_id=1, source_target_pairs={{0,24},{8,0},{16,8},{24,16},{1,25},{9,1},{17,9},{25,17},{2,26},{10... | collective-permute-start | bytes 233480 | tf_op jit(solution)/shard_map/ppermute | solution.py:406
  14.5 7.7 %copy-start.2 = (s32[4,64,128]{2,1,0:T(8,128)S(1)}, s32[4,64,128]{2,1,0:T(8,128)}, u32[]{:S(2)}) copy-start(s32[4,64,128]{2,1,0:T(8,128)} %codes.5) | copy-start | bytes 393220
  14.5 7.7 %copy-start.7 = (s32[64,128]{1,0:T(8,128)S(1)}, s32[64,128]{1,0:T(8,128)}, u32[]{:S(2)}) copy-start(s32[64,128]{1,0:T(8,128)} %groups.5) | copy-start | bytes 98308
  15.2 6.3 %collective-permute-start.3 = (f32[184,128]{1,0:T(8,128)S(1)}, f32[184,128]{1,0:T(8,128)S(1)}, u32[]{:S(2)}, u32[]{:S(2)}) collective-permute-start(f32[184,128]{1,0:T(8,128)S(1)} %get-tuple-element.56), channel_id=1, source_target_pairs={{0,2},{2,4},{4,6},{6,0},{1,3},{3,5},{5,7},{7,1},{8,10},{10,12},{12... | collective-permute-start | bytes 282632 | tf_op jit(solution)/shard_map/ppermute | solution.py:406
  16.7 5.5 %collective-permute-start.4 = (f32[184,128]{1,0:T(8,128)S(1)}, f32[184,128]{1,0:T(8,128)S(1)}, u32[]{:S(2)}, u32[]{:S(2)}) collective-permute-start(f32[184,128]{1,0:T(8,128)S(1)} %get-tuple-element.57), channel_id=1, source_target_pairs={{0,6},{2,0},{4,2},{6,4},{1,7},{3,1},{5,3},{7,5},{8,14},{10,8},{12,... | collective-permute-start | bytes 282632 | tf_op jit(solution)/shard_map/ppermute | solution.py:406
  22.2 0.7 copy-start.8
  33.3 1.2 %collective-permute-start.5 = (f32[3,8,128]{2,1,0:T(8,128)S(1)}, f32[3,8,128]{2,1,0:T(8,128)S(1)}, u32[]{:S(2)}, u32[]{:S(2)}) collective-permute-start(f32[3,8,128]{2,1,0:T(8,128)S(1)} %get-tuple-element.59), channel_id=1, source_target_pairs={{0,1},{1,0},{2,3},{3,2},{4,5},{5,4},{6,7},{7,6},{8,9},{9,8},{10,11... | collective-permute-start | bytes 36872 | tf_op jit(solution)/shard_map/ppermute | solution.py:406
  35.2 5.8 %collective-permute-start.6 = (f32[3,24,128]{2,1,0:T(8,128)S(1)}, f32[3,24,128]{2,1,0:T(8,128)S(1)}, u32[]{:S(2)}, u32[]{:S(2)}) collective-permute-start(f32[3,24,128]{2,1,0:T(8,128)S(1)} %get-tuple-element.62), channel_id=1, source_target_pairs={{0,8},{8,16},{16,24},{24,0},{1,9},{9,17},{17,25},{25,1},{2,10},{10... | collective-permute-start | bytes 110600 | tf_op jit(solution)/shard_map/ppermute | solution.py:406
  36.9 4.4 %collective-permute-start.7 = (f32[3,24,128]{2,1,0:T(8,128)S(1)}, f32[3,24,128]{2,1,0:T(8,128)S(1)}, u32[]{:S(2)}, u32[]{:S(2)}) collective-permute-start(f32[3,24,128]{2,1,0:T(8,128)S(1)} %get-tuple-element.63), channel_id=1, source_target_pairs={{0,24},{8,0},{16,8},{24,16},{1,25},{9,1},{17,9},{25,17},{2,26},{10... | collective-permute-start | bytes 110600 | tf_op jit(solution)/shard_map/ppermute | solution.py:406
  41.9 4.9 %collective-permute-start.8 = (f32[3,24,128]{2,1,0:T(8,128)S(1)}, f32[3,24,128]{2,1,0:T(8,128)S(1)}, u32[]{:S(2)}, u32[]{:S(2)}) collective-permute-start(f32[3,24,128]{2,1,0:T(8,128)S(1)} %get-tuple-element.66), channel_id=1, source_target_pairs={{0,2},{2,4},{4,6},{6,0},{1,3},{3,5},{5,7},{7,1},{8,10},{10,12},{12... | collective-permute-start | bytes 110600 | tf_op jit(solution)/shard_map/ppermute | solution.py:406
  43.4 4.0 %collective-permute-start.9 = (f32[3,24,128]{2,1,0:T(8,128)S(1)}, f32[3,24,128]{2,1,0:T(8,128)S(1)}, u32[]{:S(2)}, u32[]{:S(2)}) collective-permute-start(f32[3,24,128]{2,1,0:T(8,128)S(1)} %get-tuple-element.67), channel_id=1, source_target_pairs={{0,6},{2,0},{4,2},{6,4},{1,7},{3,1},{5,3},{7,5},{8,14},{10,8},{12,... | collective-permute-start | bytes 110600 | tf_op jit(solution)/shard_map/ppermute | solution.py:406
  56.7 1.2 %collective-permute-start.10 = (f32[3,8,128]{2,1,0:T(8,128)S(1)}, f32[3,8,128]{2,1,0:T(8,128)S(1)}, u32[]{:S(2)}, u32[]{:S(2)}) collective-permute-start(f32[3,8,128]{2,1,0:T(8,128)S(1)} %get-tuple-element.73), channel_id=1, source_target_pairs={{0,1},{1,0},{2,3},{3,2},{4,5},{5,4},{6,7},{7,6},{8,9},{9,8},{10,11... | collective-permute-start | bytes 36872 | tf_op jit(solution)/shard_map/ppermute | solution.py:406
  58.6 5.8 %collective-permute-start.11 = (f32[3,24,128]{2,1,0:T(8,128)S(1)}, f32[3,24,128]{2,1,0:T(8,128)S(1)}, u32[]{:S(2)}, u32[]{:S(2)}) collective-permute-start(f32[3,24,128]{2,1,0:T(8,128)S(1)} %get-tuple-element.76), channel_id=1, source_target_pairs={{0,8},{8,16},{16,24},{24,0},{1,9},{9,17},{17,25},{25,1},{2,10},{10... | collective-permute-start | bytes 110600 | tf_op jit(solution)/shard_map/ppermute | solution.py:406
  58.7 5.7 %collective-permute-start.12 = (f32[3,24,128]{2,1,0:T(8,128)S(1)}, f32[3,24,128]{2,1,0:T(8,128)S(1)}, u32[]{:S(2)}, u32[]{:S(2)}) collective-permute-start(f32[3,24,128]{2,1,0:T(8,128)S(1)} %get-tuple-element.77), channel_id=1, source_target_pairs={{0,24},{8,0},{16,8},{24,16},{1,25},{9,1},{17,9},{25,17},{2,26},{10... | collective-permute-start | bytes 110600 | tf_op jit(solution)/shard_map/ppermute | solution.py:406
  65.0 4.9 %collective-permute-start.13 = (f32[3,24,128]{2,1,0:T(8,128)S(1)}, f32[3,24,128]{2,1,0:T(8,128)S(1)}, u32[]{:S(2)}, u32[]{:S(2)}) collective-permute-start(f32[3,24,128]{2,1,0:T(8,128)S(1)} %get-tuple-element.80), channel_id=1, source_target_pairs={{0,2},{2,4},{4,6},{6,0},{1,3},{3,5},{5,7},{7,1},{8,10},{10,12},{12... | collective-permute-start | bytes 110600 | tf_op jit(solution)/shard_map/ppermute | solution.py:406
  66.5 4.0 %collective-permute-start.14 = (f32[3,24,128]{2,1,0:T(8,128)S(1)}, f32[3,24,128]{2,1,0:T(8,128)S(1)}, u32[]{:S(2)}, u32[]{:S(2)}) collective-permute-start(f32[3,24,128]{2,1,0:T(8,128)S(1)} %get-tuple-element.81), channel_id=1, source_target_pairs={{0,6},{2,0},{4,2},{6,4},{1,7},{3,1},{5,3},{7,5},{8,14},{10,8},{12,... | collective-permute-start | bytes 110600 | tf_op jit(solution)/shard_map/ppermute | solution.py:406
  79.8 1.2 %collective-permute-start.15 = (f32[3,8,128]{2,1,0:T(8,128)S(1)}, f32[3,8,128]{2,1,0:T(8,128)S(1)}, u32[]{:S(2)}, u32[]{:S(2)}) collective-permute-start(f32[3,8,128]{2,1,0:T(8,128)S(1)} %get-tuple-element.84), channel_id=1, source_target_pairs={{0,1},{1,0},{2,3},{3,2},{4,5},{5,4},{6,7},{7,6},{8,9},{9,8},{10,11... | collective-permute-start | bytes 36872 | tf_op jit(solution)/shard_map/ppermute | solution.py:406
  81.7 5.8 %collective-permute-start.16 = (f32[3,24,128]{2,1,0:T(8,128)S(1)}, f32[3,24,128]{2,1,0:T(8,128)S(1)}, u32[]{:S(2)}, u32[]{:S(2)}) collective-permute-start(f32[3,24,128]{2,1,0:T(8,128)S(1)} %get-tuple-element.87), channel_id=1, source_target_pairs={{0,8},{8,16},{16,24},{24,0},{1,9},{9,17},{17,25},{25,1},{2,10},{10... | collective-permute-start | bytes 110600 | tf_op jit(solution)/shard_map/ppermute | solution.py:406
  82.9 4.7 %collective-permute-start.17 = (f32[3,24,128]{2,1,0:T(8,128)S(1)}, f32[3,24,128]{2,1,0:T(8,128)S(1)}, u32[]{:S(2)}, u32[]{:S(2)}) collective-permute-start(f32[3,24,128]{2,1,0:T(8,128)S(1)} %get-tuple-element.88), channel_id=1, source_target_pairs={{0,24},{8,0},{16,8},{24,16},{1,25},{9,1},{17,9},{25,17},{2,26},{10... | collective-permute-start | bytes 110600 | tf_op jit(solution)/shard_map/ppermute | solution.py:406
  88.3 4.9 %collective-permute-start.18 = (f32[3,24,128]{2,1,0:T(8,128)S(1)}, f32[3,24,128]{2,1,0:T(8,128)S(1)}, u32[]{:S(2)}, u32[]{:S(2)}) collective-permute-start(f32[3,24,128]{2,1,0:T(8,128)S(1)} %get-tuple-element.91), channel_id=1, source_target_pairs={{0,2},{2,4},{4,6},{6,0},{1,3},{3,5},{5,7},{7,1},{8,10},{10,12},{12... | collective-permute-start | bytes 110600 | tf_op jit(solution)/shard_map/ppermute | solution.py:406
  89.6 4.0 %collective-permute-start.19 = (f32[3,24,128]{2,1,0:T(8,128)S(1)}, f32[3,24,128]{2,1,0:T(8,128)S(1)}, u32[]{:S(2)}, u32[]{:S(2)}) collective-permute-start(f32[3,24,128]{2,1,0:T(8,128)S(1)} %get-tuple-element.92), channel_id=1, source_target_pairs={{0,6},{2,0},{4,2},{6,4},{1,7},{3,1},{5,3},{7,5},{8,14},{10,8},{12,... | collective-permute-start | bytes 110600 | tf_op jit(solution)/shard_map/ppermute | solution.py:406
